TPU v7x, 128 devices: a whole 4x4x4 slice. The times are simulated.
128 devices in a mesh: dp: 8 (over y, core), row: 2 (over z_lo), col: 8 (over x, z_hi).
Axes of the slice: x: 4, y: 4, z: 4 (z_hi: 2, z_lo: 2; z = z_hi * 2 + z_lo), core: 2. Of those that a mesh axis runs over, the one named last changes fastest.
Arguments:
- hidden_in: float32 [2048, 1024], P('dp', 'row'), may hold values from -6 to 6
- cotangent: float32 [2048, 1024], P('dp', 'row'), may hold values from -6 to 6
- norm_gains: float32 [2, 2, 1024], P(None, None, 'row'), may hold values from 0.1 to 1.9
- query_key_value_weight: bfloat16 [2, 1024, 2048], P(None, 'row', 'col'), may hold values from -0.1875 to 0.1875
- w_out: bfloat16 [2, 1024, 1024], P(None, 'col', 'row'), may hold values from -0.75 to 0.75
- w_router: bfloat16 [2, 1024, 32], P(None, 'row', 'col'), may hold values from -0.1875 to 0.1875
- w_gate_up: bfloat16 [2, 32, 1024, 1024], P(None, 'col', 'row'), may hold values from -0.1875 to 0.1875
- w_down: bfloat16 [2, 32, 512, 1024], P(None, 'col', None, 'row'), may hold values from -0.75 to 0.75
- expert_ids: int32 [2, 2048, 8], P(None, 'dp'), may hold values from 0 to 31, all different within a row; in each aligned block of 256 rows (0 to 255, 256 to 511, ..., all dimensions but the last counted through in order) at most 128 rows name the same one
Outputs:
- block_out: float32 [2048, 1024], P('dp', 'row')
- grad_hidden: float32 [2048, 1024], P('dp', 'row')
- grad_gains: float32 [2, 2, 1024], P(None, None, ('row', 'dp'))
- grad_qkv: float32 [2, 1024, 2048], P(None, ('row', 'dp'), 'col')
- grad_out: float32 [2, 1024, 1024], P(None, ('col', 'dp'), 'row')
- grad_router: float32 [2, 1024, 32], P(None, ('row', 'dp'), 'col')
- grad_gate_up: float32 [2, 32, 1024, 1024], P(None, 'col', ('row', 'dp'))
- grad_down: float32 [2, 32, 512, 1024], P(None, 'col', 'dp', 'row')
Inputs may be any that keep to these rules, and one draw needn't show every extreme that they name: `expert_ids`: each token names 8 different experts in each layer. Among the 256 tokens of one index of dp in one layer, no expert is named by more than 128 tokens, a bound that some block reaches.
All inputs are finite; a program needn't handle non-finite values.
Results may differ from a plain program's by a relative error of at most 0.04.
Values may be sent and summed in bfloat16 or wider, within the bound.
No kernel may reach another device: no remote copies, remote signals or barrier semaphores. Data moves between devices by JAX's collectives and lax.ppermute only.
A program may use at most 128 MiB of HBM per device.

v0:
```python
import jax
import jax.numpy as jnp
from jax import lax
from jax.experimental import pallas as pl
from jax.experimental.pallas import tpu as pltpu
from jax.sharding import PartitionSpec as P

MODEL_WIDTH = 1024
HALF = 512
HEAD_SIZE = 64
FF = 512
TOKENS = 256
PEERS = 16
OWN_TOKENS = 16
N_DP = 8
NORM_EPS = 1e-06
ROPE_BASE = 10000.0
GROUP = ("row", "col")
F32 = jnp.float32
BF16 = jnp.bfloat16


def dot(a, b, dims):
    return lax.dot_general(a, b, (dims, ((), ())), preferred_element_type=F32)


def mm(a, b):
    return dot(a, b, ((1,), (0,)))


def mm_nt(a, b):
    return dot(a, b, ((1,), (1,)))


def mm_tn(a, b):
    return dot(a, b, ((0,), (0,)))


def row_swap(value):
    return lax.ppermute(value, "row", [(0, 1), (1, 0)])


def swap_halves(value):
    return jnp.concatenate([value[..., HALF:MODEL_WIDTH], value[..., :HALF]], axis=-1)


def split_two(value):
    high = lax.reduce_precision(value, 8, 7)
    return (high.astype(BF16), (value - high).astype(BF16))


def rope_tables():
    half_width = HEAD_SIZE // 2
    frequency = ROPE_BASE ** (-2.0 * jnp.arange(half_width, dtype=F32) / HEAD_SIZE)
    angles = jnp.arange(TOKENS, dtype=F32)[:, None] * frequency[None, :]
    return (jnp.tile(jnp.cos(angles), (1, 4)), jnp.tile(jnp.sin(angles), (1, 4)))


def halves_swapped(pair, sign):
    lane = lax.broadcasted_iota(jnp.int32, pair.shape, 1) % HEAD_SIZE
    half = HEAD_SIZE // 2
    up = pltpu.roll(pair, 128 - half, 1)
    down = pltpu.roll(pair, half, 1)
    return jnp.where(lane < half, -sign * up, sign * down)


def causal():
    return lax.broadcasted_iota(jnp.int32, (TOKENS, TOKENS), 0) >= lax.broadcasted_iota(
        jnp.int32, (TOKENS, TOKENS), 1
    )


def whole(shape):
    zeros = (0,) * len(shape)
    return pl.BlockSpec(shape, lambda *_: zeros)


def at_layer(shape, layer):
    zeros = (0,) * (len(shape))
    return pl.BlockSpec((None,) + shape, lambda *_: (layer,) + zeros)


def shaped(shape, dtype):
    return jax.ShapeDtypeStruct(shape, dtype)


def cost(flops, size):
    return pl.CostEstimate(flops=flops, bytes_accessed=size, transcendentals=0)


def tokens_of(ref):
    return ref[:, :, :MODEL_WIDTH].reshape(TOKENS, MODEL_WIDTH)


def attend_kernel(x_ref, heads_ref, out_ref, cos_ref, sin_ref, part_ref, qkv_ref, att_ref, lse_ref):
    qkv = mm(tokens_of(x_ref), heads_ref[...])
    pair = qkv[:, :128]
    pair = (pair * cos_ref[...] + halves_swapped(pair, 1.0) * sin_ref[...]).astype(BF16)
    value = qkv[:, 128:].astype(BF16)
    scores = mm_nt(pair[:, :HEAD_SIZE], pair[:, HEAD_SIZE:]) * (1.0 / HEAD_SIZE)
    allowed = causal()
    total = jnp.log(jnp.sum(jnp.where(allowed, jnp.exp(scores), 0.0), axis=1, keepdims=True))
    probs = jnp.where(allowed, jnp.exp(scores - total), 0.0).astype(BF16)
    attended = mm(probs, value).astype(BF16)
    part = mm(attended, out_ref[...]).astype(BF16)
    part_ref[...] = part.reshape(PEERS, OWN_TOKENS, MODEL_WIDTH)
    qkv_ref[:, :128] = pair
    qkv_ref[:, 128:] = value
    att_ref[...] = attended
    lse_ref[...] = total


def attend(got, heads, out_rows, cosine, sine, layer):
    return pl.pallas_call(
        attend_kernel,
        name="attend",
        grid=(1,),
        in_specs=[
            whole(got.shape),
            at_layer(heads.shape[1:], layer),
            at_layer(out_rows.shape[1:], layer),
            whole(cosine.shape),
            whole(sine.shape),
        ],
        out_specs=[
            whole((PEERS, OWN_TOKENS, MODEL_WIDTH)),
            whole((TOKENS, 192)),
            whole((TOKENS, HEAD_SIZE)),
            whole((TOKENS, 1)),
        ],
        out_shape=[
            shaped((PEERS, OWN_TOKENS, MODEL_WIDTH), BF16),
            shaped((TOKENS, 192), BF16),
            shaped((TOKENS, HEAD_SIZE), BF16),
            shaped((TOKENS, 1), F32),
        ],
        cost_estimate=cost(200_000_000, 2_000_000),
    )(got, heads, out_rows, cosine, sine)


def attend_back_kernel(
    row_ref, low_ref, x_ref, heads_ref, out_ref, cos_ref, sin_ref, qkv_ref, att_ref, lse_ref,
    router_ref, gain_ref, send_ref, small_ref, sum_ref, pair_ref, cols_ref,
):
    lower = row_ref[0] == 0
    low = tokens_of(low_ref)
    sum_ref[...] = jnp.sum(low_ref[:, :, MODEL_WIDTH:].astype(F32), axis=0)
    query, key = qkv_ref[:, :HEAD_SIZE], qkv_ref[:, HEAD_SIZE:128]
    value = qkv_ref[:, 128:]
    attended = att_ref[...]
    grad_attended = mm_nt(low, out_ref[...]).astype(BF16)
    grad_out = mm_tn(attended, low)
    scores = mm_nt(query, key) * (1.0 / HEAD_SIZE)
    probs = jnp.where(causal(), jnp.exp(scores - lse_ref[...]), 0.0)
    grad_value = mm_tn(probs.astype(BF16), grad_attended)
    grad_probs = mm_nt(grad_attended, value)
    delta = jnp.sum(grad_attended.astype(F32) * attended.astype(F32), axis=1, keepdims=True)
    grad_scores = (probs * (grad_probs - delta) * (1.0 / HEAD_SIZE)).astype(BF16)
    pair_ref[:, :HEAD_SIZE] = mm(grad_scores, key)
    pair_ref[:, HEAD_SIZE:] = mm_tn(grad_scores, query)
    pair = pair_ref[...]
    pair = pair * cos_ref[...] + halves_swapped(pair * sin_ref[...], -1.0)
    cols_ref[:, :128] = pair.astype(BF16)
    cols_ref[:, 128:] = grad_value.astype(BF16)
    columns = cols_ref[...]
    part = mm_nt(columns, heads_ref[...]).astype(BF16)
    send_ref[:, :, :MODEL_WIDTH] = part.reshape(PEERS, OWN_TOKENS, MODEL_WIDTH)
    grad_heads = mm_tn(tokens_of(x_ref), columns)
    product = grad_heads * heads_ref[...].astype(F32)
    gain = lax.dot_general(
        jnp.ones((8, 192), F32),
        product,
        (((1,), (1,)), ((), ())),
        preferred_element_type=F32,
        precision=lax.Precision.HIGHEST,
    )[:1]
    gain = jnp.where(lower, gain, swap_halves(gain)) / gain_ref[...]
    high = gain.astype(BF16)
    rest = (gain - high.astype(F32)).astype(BF16)
    for j in range(8):
        lanes = slice(128 * j, 128 * j + 128)
        wide = slice(MODEL_WIDTH, MODEL_WIDTH + 128)
        send_ref[:, j : j + 1, wide] = jnp.broadcast_to(high[:, lanes][None], (PEERS, 1, 128))
        send_ref[:, 8 + j : 9 + j, wide] = jnp.broadcast_to(rest[:, lanes][None], (PEERS, 1, 128))
    query_part = grad_heads[:, :HEAD_SIZE].astype(BF16)
    rest_part = grad_heads[:, HEAD_SIZE:].astype(BF16)
    blank = jnp.zeros_like(query_part)
    slot_a = jnp.where(lower, query_part, blank)
    slot_b = jnp.where(lower, blank, query_part)
    router = router_ref[...].astype(BF16)
    grad_out = grad_out.astype(BF16)
    for k in range(N_DP):
        mine = (k // 4 == 0) == lower
        small_ref[k, 128:, :] = jnp.zeros((16, 512), BF16)
        for half in range(2):
            rows = slice(half * HALF + 64 * k, half * HALF + 64 * k + 64)
            to = slice(64 * half, 64 * half + 64)
            small_ref[k, to, :64] = slot_a[rows]
            small_ref[k, to, 64:128] = slot_b[rows]
            small_ref[k, to, 128:256] = rest_part[rows]
            small_ref[k, to, 384:] = jnp.zeros((64, 128), BF16)
            small_ref[k, to, 384:416] = router[rows]
            for j in range(4):
                piece = grad_out[16 * (k % 4) : 16 * (k % 4) + 16]
                piece = piece[:, half * HALF + 128 * j : half * HALF + 128 * j + 128]
                small_ref[k, 64 * half + 16 * j : 64 * half + 16 * j + 16, 256:384] = jnp.where(
                    mine, piece, jnp.zeros_like(piece)
                )


def attend_back(row, low, got, heads, out_rows, cosine, sine, saved, router_grad, gain, layer):
    qkv, attended, total = saved
    send = (PEERS, OWN_TOKENS, MODEL_WIDTH + 128)
    return pl.pallas_call(
        attend_back_kernel,
        name="attend_back",
        grid_spec=pltpu.PrefetchScalarGridSpec(
            num_scalar_prefetch=1,
            grid=(1,),
            in_specs=[
                whole(low.shape),
                whole(got.shape),
                at_layer(heads.shape[1:], layer),
                at_layer(out_rows.shape[1:], layer),
                whole(cosine.shape),
                whole(sine.shape),
                whole(qkv.shape),
                whole(attended.shape),
                whole(total.shape),
                whole(router_grad.shape),
                whole((1, MODEL_WIDTH)),
            ],
            out_specs=[whole(send), whole((N_DP, 144, 512)), whole((OWN_TOKENS, 128))],
            scratch_shapes=[pltpu.VMEM((TOKENS, 128), F32), pltpu.VMEM((TOKENS, 192), BF16)],
        ),
        out_shape=[
            shaped(send, BF16),
            shaped((N_DP, 144, 512), BF16),
            shaped((OWN_TOKENS, 128), F32),
        ],
        cost_estimate=cost(500_000_000, 4_000_000),
    )(row, low, got, heads, out_rows, cosine, sine, qkv, attended, total, router_grad, gain)


def gate_column(gates, first, step):
    experts = lax.broadcasted_iota(jnp.int32, gates.shape, 1)
    return jnp.sum(jnp.where(experts == first + step, gates, 0.0), axis=1, keepdims=True)


def experts_kernel(
    info_ref, x_ref, router_ref, ids_ref, up_ref, down_ref, other_ref,
    part_ref, pre_ref, gates_ref, sum_ref,
):
    step = pl.program_id(0)
    x = tokens_of(x_ref)

    @pl.when(step == 0)
    def _():
        logits = mm_nt(x, router_ref[...])
        experts = lax.broadcasted_iota(jnp.int32, logits.shape, 1)
        ids = ids_ref[...]
        chosen = ids[:, 0:1] == experts
        for j in range(1, 8):
            chosen = chosen | (ids[:, j : j + 1] == experts)
        exponent = jnp.where(chosen, jnp.exp(logits), 0.0)
        gates_ref[...] = exponent / jnp.sum(exponent, axis=1, keepdims=True)

    pre = mm(x[:, :HALF], up_ref[...]) + mm(x[:, HALF:], other_ref[:, : 2 * FF])
    pre_ref[...] = pre
    gate_part = pre[:, :FF]
    act = (gate_part / (1.0 + jnp.exp(-gate_part)) * pre[:, FF:]).astype(BF16)
    gate = gate_column(gates_ref[...], info_ref[1], step)
    left = gate * mm(act, down_ref[...])
    right = gate * mm(act, other_ref[:, 2 * FF :])

    @pl.when(step == 0)
    def _():
        sum_ref[:, :HALF] = left
        sum_ref[:, HALF:] = right

    @pl.when(step == 1)
    def _():
        shape = (PEERS, OWN_TOKENS, HALF)
        part_ref[:, :, :HALF] = (sum_ref[:, :HALF] + left).astype(BF16).reshape(shape)
        part_ref[:, :, HALF:] = (sum_ref[:, HALF:] + right).astype(BF16).reshape(shape)


def weight_specs(layer):
    return [
        pl.BlockSpec((None, None, HALF, 2 * FF), lambda e, info: (layer, 2 * info[0] + e, 0, 0)),
        pl.BlockSpec((None, None, FF, HALF), lambda e, info: (layer, 2 * info[0] + e, 0, 0)),
        pl.BlockSpec((HALF, 3 * HALF), lambda e, info: (e, 0)),
    ]


def experts(info, got, router, ids, w_up, w_down, other, layer):
    send = (PEERS, OWN_TOKENS, MODEL_WIDTH)
    return pl.pallas_call(
        experts_kernel,
        name="experts",
        grid_spec=pltpu.PrefetchScalarGridSpec(
            num_scalar_prefetch=1,
            grid=(2,),
            in_specs=[whole(got.shape), whole(router.shape), at_layer((TOKENS, 8), layer)]
            + weight_specs(layer),
            out_specs=[
                whole(send),
                pl.BlockSpec((None, TOKENS, 2 * FF), lambda e, info: (e, 0, 0)),
                whole((TOKENS, 32)),
            ],
            scratch_shapes=[pltpu.VMEM((TOKENS, MODEL_WIDTH), F32)],
        ),
        out_shape=[
            shaped(send, BF16),
            shaped((2, TOKENS, 2 * FF), F32),
            shaped((TOKENS, 32), F32),
        ],
        cost_estimate=cost(1_600_000_000, 9_000_000),
    )(info, got, router, ids, w_up, w_down, other)


def experts_back_kernel(
    info_ref, g_ref, mean_ref, gates_ref, pre_ref, router_ref, up_ref, down_ref, other_ref,
    part_ref, grad_pre_ref, act_ref, grad_y_ref, logit_ref, sum_ref,
):
    step = pl.program_id(0)
    upstream = g_ref[...]
    mean_cols = mean_ref[...].astype(F32)
    mean = mean_cols[:, :1] + mean_cols[:, 1:2]
    gates = gates_ref[...]
    gate = gate_column(gates, info_ref[1], step)
    gate_part, up_part = pre_ref[:, :FF], pre_ref[:, FF:]
    sig = 1.0 / (1.0 + jnp.exp(-gate_part))
    act = (gate_part * sig * up_part).astype(BF16)
    act_ref[...] = act
    raw = mm_nt(upstream[:, :HALF], down_ref[...])
    raw = raw + mm_nt(upstream[:, HALF:], other_ref[:, 2 * FF :])
    grad_gate = jnp.sum(act.astype(F32) * raw, axis=1, keepdims=True)
    back = gate * raw
    left = (back * up_part * sig * (1.0 + gate_part * (1.0 - sig))).astype(BF16)
    right = (back * gate_part * sig).astype(BF16)
    grad_pre_ref[:, :FF] = left
    grad_pre_ref[:, FF:] = right
    grad_pre = grad_pre_ref[...]
    grad_y_ref[...] = (gate * upstream.astype(F32)).astype(BF16)
    column = (gate * (grad_gate - mean)).astype(BF16).astype(F32)
    experts_at = lax.broadcasted_iota(jnp.int32, gates.shape, 1) == info_ref[1] + step
    low = mm_nt(grad_pre, up_ref[...])
    high = mm_nt(grad_pre, other_ref[:, : 2 * FF])

    @pl.when(step == 0)
    def _():
        logit_ref[...] = jnp.where(experts_at, column, 0.0)
        sum_ref[:, :HALF] = low
        sum_ref[:, HALF:] = high

    @pl.when(step == 1)
    def _():
        logits = jnp.where(experts_at, column, logit_ref[...])
        logit_ref[...] = logits
        routed = mm(logits.astype(BF16), router_ref[...])
        shape = (PEERS, OWN_TOKENS, HALF)
        low_sum = sum_ref[:, :HALF] + low + routed[:, :HALF]
        high_sum = sum_ref[:, HALF:] + high + routed[:, HALF:]
        part_ref[:, :, :HALF] = low_sum.astype(BF16).reshape(shape)
        part_ref[:, :, HALF:] = high_sum.astype(BF16).reshape(shape)


def experts_back(info, upstream, mean, gates, pre, router, w_up, w_down, other, layer):
    send = (PEERS, OWN_TOKENS, MODEL_WIDTH)

    def per_expert(width):
        return pl.BlockSpec((None, TOKENS, width), lambda e, info: (e, 0, 0))

    return pl.pallas_call(
        experts_back_kernel,
        name="experts_back",
        grid_spec=pltpu.PrefetchScalarGridSpec(
            num_scalar_prefetch=1,
            grid=(2,),
            in_specs=[
                whole(upstream.shape),
                whole(mean.shape),
                whole(gates.shape),
                per_expert(2 * FF),
                whole(router.shape),
            ]
            + weight_specs(layer),
            out_specs=[
                whole(send),
                per_expert(2 * FF),
                per_expert(FF),
                per_expert(MODEL_WIDTH),
                whole((TOKENS, 32)),
            ],
            scratch_shapes=[pltpu.VMEM((TOKENS, MODEL_WIDTH), F32)],
        ),
        out_shape=[
            shaped(send, BF16),
            shaped((2, TOKENS, 2 * FF), BF16),
            shaped((2, TOKENS, FF), BF16),
            shaped((2, TOKENS, MODEL_WIDTH), BF16),
            shaped((TOKENS, 32), F32),
        ],
        cost_estimate=cost(1_700_000_000, 11_000_000),
    )(info, upstream, mean, gates, pre, router, w_up, w_down, other)


def experts_grads_kernel(x_ref, grad_pre_ref, act_ref, grad_y_ref, logit_ref, pack_ref, router_ref):
    x = tokens_of(x_ref)
    up = mm_tn(x, grad_pre_ref[...]).astype(BF16)
    down = mm_tn(act_ref[...], grad_y_ref[...]).astype(BF16)
    for k in range(N_DP):
        pack_ref[k, :64] = up[64 * k : 64 * k + 64]
        pack_ref[k, 64:128] = up[HALF + 64 * k : HALF + 64 * k + 64]
        pack_ref[k, 128:] = down[64 * k : 64 * k + 64]

    @pl.when(pl.program_id(0) == 0)
    def _():
        router_ref[...] = mm_tn(x, logit_ref[...].astype(BF16))


def experts_grads(got, grad_pre, act, grad_y, logits):
    def per_expert(width):
        return pl.BlockSpec((None, TOKENS, width), lambda e: (e, 0, 0))

    return pl.pallas_call(
        experts_grads_kernel,
        name="experts_grads",
        grid=(2,),
        in_specs=[
            whole(got.shape),
            per_expert(2 * FF),
            per_expert(FF),
            per_expert(MODEL_WIDTH),
            whole(logits.shape),
        ],
        out_specs=[
            pl.BlockSpec((N_DP, 192, MODEL_WIDTH), lambda e: (0, e, 0)),
            whole((MODEL_WIDTH, 32)),
        ],
        out_shape=[shaped((N_DP, 384, MODEL_WIDTH), BF16), shaped((MODEL_WIDTH, 32), F32)],
        cost_estimate=cost(1_600_000_000, 9_000_000),
    )(got, grad_pre, act, grad_y, logits)


def summed(got_ref):
    first = got_ref[0, :, :MODEL_WIDTH].astype(F32)
    second = got_ref[8, :, :MODEL_WIDTH].astype(F32)
    for j in range(1, 8):
        first = first + got_ref[j, :, :MODEL_WIDTH].astype(F32)
        second = second + got_ref[8 + j, :, :MODEL_WIDTH].astype(F32)
    return first + swap_halves(second)


def put_rows(send_ref, rows):
    rows = rows.astype(BF16)
    swapped = swap_halves(rows)
    for j in range(8):
        send_ref[j, :, :MODEL_WIDTH] = rows
        send_ref[8 + j, :, :MODEL_WIDTH] = swapped


def put_halves(send_ref, rows):
    rows = rows.astype(BF16)
    for j in range(8):
        send_ref[j, :, :HALF] = rows[:, :HALF]
        send_ref[8 + j, :, :HALF] = rows[:, HALF:]


def put_extra(send_ref, extra, start):
    for j in range(PEERS):
        send_ref[j, :, start:] = extra


def pair_columns(column):
    high = column.astype(BF16).astype(F32)
    lane = lax.broadcasted_iota(jnp.int32, (OWN_TOKENS, 128), 1)
    wide = jnp.where(lane == 0, high, jnp.where(lane == 1, column - high, 0.0))
    return wide.astype(BF16)


def scale_of(hidden):
    return lax.rsqrt(jnp.mean(hidden * hidden, axis=1, keepdims=True) + NORM_EPS)


def add_norm_kernel(got_ref, base_ref, gain_ref, *rest):
    *extra, total_ref, sum_ref, send_ref = rest
    part = summed(got_ref)
    total = base_ref[...] + part
    total_ref[...] = total
    sum_ref[...] = part
    put_rows(send_ref, total * scale_of(total) * gain_ref[...])
    if extra:
        put_extra(send_ref, extra[0][...], MODEL_WIDTH)


def add_norm(got, base, gain, extra=None):
    width = MODEL_WIDTH + (0 if extra is None else extra.shape[1])
    rows = shaped((OWN_TOKENS, MODEL_WIDTH), F32)
    return pl.pallas_call(
        add_norm_kernel,
        name="add_norm",
        out_shape=[rows, rows, shaped((PEERS, OWN_TOKENS, width), BF16)],
        cost_estimate=cost(1_000_000, 1_000_000),
    )(got, base, gain, *([] if extra is None else [extra]))


def add_last_kernel(got_ref, base_ref, grad_ref, sum_ref, send_ref):
    part = summed(got_ref)
    sum_ref[...] = part
    put_halves(send_ref, base_ref[...] + part)
    mean = jnp.sum(grad_ref[...] * part, axis=1, keepdims=True)
    put_extra(send_ref, pair_columns(mean), HALF)


def add_last(got, base, grad):
    return pl.pallas_call(
        add_last_kernel,
        name="add_last",
        out_shape=[
            shaped((OWN_TOKENS, MODEL_WIDTH), F32),
            shaped((PEERS, OWN_TOKENS, HALF + 128), BF16),
        ],
        cost_estimate=cost(1_000_000, 1_000_000),
    )(got, base, grad)


def back_through_norm(hidden, gain, grad_normed):
    scaling = scale_of(hidden)
    weighted = grad_normed * gain
    inner = jnp.sum(weighted * hidden, axis=1, keepdims=True)
    return scaling * weighted - hidden * (scaling**3 * inner * (1.0 / MODEL_WIDTH))


def middle_back_kernel(got_ref, hidden_ref, gain_ref, grad_ref, out_ref, send_ref):
    grad_normed = summed(got_ref)
    hidden = hidden_ref[...]
    grad = grad_ref[...] + back_through_norm(hidden, gain_ref[...], grad_normed)
    out_ref[...] = grad
    put_rows(send_ref, grad)
    gain = jnp.sum(grad_normed * hidden * scale_of(hidden), axis=0, keepdims=True)
    high = gain.astype(BF16)
    rest = (gain - high.astype(F32)).astype(BF16)
    wide = slice(MODEL_WIDTH, MODEL_WIDTH + 128)
    for j in range(8):
        lanes = slice(128 * j, 128 * j + 128)
        send_ref[:, j : j + 1, wide] = jnp.broadcast_to(high[:, lanes][None], (PEERS, 1, 128))
        send_ref[:, 8 + j : 9 + j, wide] = jnp.broadcast_to(rest[:, lanes][None], (PEERS, 1, 128))


def middle_back(got, hidden, gain, grad):
    return pl.pallas_call(
        middle_back_kernel,
        name="middle_back",
        out_shape=[
            shaped((OWN_TOKENS, MODEL_WIDTH), F32),
            shaped((PEERS, OWN_TOKENS, MODEL_WIDTH + 128), BF16),
        ],
        cost_estimate=cost(1_000_000, 1_000_000),
    )(got, hidden, gain, grad)


def first_back_kernel(got_ref, hidden_ref, gain_ref, grad_ref, *rest):
    *mixed, out_ref, sum_ref, send_ref = rest
    hidden = hidden_ref[...]
    grad = grad_ref[...] + back_through_norm(hidden, gain_ref[...], summed(got_ref))
    out_ref[...] = grad
    sum_ref[...] = jnp.sum(got_ref[:, :, MODEL_WIDTH:].astype(F32), axis=0)
    if mixed:
        put_rows(send_ref, grad)
        mean = jnp.sum(grad * mixed[0][...], axis=1, keepdims=True)
        put_extra(send_ref, pair_columns(mean), MODEL_WIDTH)
    else:
        put_halves(send_ref, grad)


def first_back(got, hidden, gain, grad, mixed=None):
    width = HALF if mixed is None else MODEL_WIDTH + 128
    return pl.pallas_call(
        first_back_kernel,
        name="first_back",
        out_shape=[
            shaped((OWN_TOKENS, MODEL_WIDTH), F32),
            shaped((OWN_TOKENS, 128), F32),
            shaped((PEERS, OWN_TOKENS, width), BF16),
        ],
        cost_estimate=cost(1_000_000, 1_000_000),
    )(got, hidden, gain, grad, *([] if mixed is None else [mixed]))


def exchange(blocks):
    return lax.all_to_all(blocks, GROUP, 0, 0, tiled=True)


def body(
    hidden_in,
    cotangent,
    norm_gains,
    query_key_value_weight,
    w_out,
    w_router,
    w_gate_up,
    w_down,
    expert_ids,
):
    r = lax.axis_index("row")
    c = lax.axis_index("col")
    lower = r == 0
    layers = 2

    def natural(own, other):
        return jnp.where(
            lower,
            jnp.concatenate([own, other], axis=-1),
            jnp.concatenate([other, own], axis=-1),
        )

    cosine, sine = rope_tables()

    gain_first = norm_gains[0, 0]
    square = jnp.sum(hidden_in * hidden_in, axis=1, keepdims=True)
    high, low = split_two(square)
    sent = jnp.concatenate(
        [
            (hidden_in * gain_first).astype(BF16),
            high,
            low,
            jnp.zeros((TOKENS, 126), BF16),
        ],
        axis=1,
    )
    got = row_swap(sent)
    square = square + got[:, HALF : HALF + 1].astype(F32) + got[:, HALF + 1 : HALF + 2].astype(F32)
    scale_all = lax.rsqrt(square / MODEL_WIDTH + NORM_EPS)
    normed_first = jnp.concatenate(
        [hidden_in * scale_all * gain_first, got[:, :HALF].astype(F32) * scale_all], axis=1
    ).astype(BF16)

    q_low = query_key_value_weight[:, :, :HEAD_SIZE]
    q_high = query_key_value_weight[:, :, HEAD_SIZE : 2 * HEAD_SIZE]
    kv = query_key_value_weight[:, :, 2 * HEAD_SIZE :]
    heads_own = jnp.concatenate([jnp.where(lower, q_low, q_high), kv], axis=2)
    heads_sent = jnp.concatenate([jnp.where(lower, q_high, q_low), kv], axis=2)
    heads = jnp.concatenate([heads_own, row_swap(heads_sent)], axis=1)
    out_low, out_high = w_out[:, :HEAD_SIZE], w_out[:, HEAD_SIZE:]
    out_rows = jnp.concatenate(
        [jnp.where(lower, out_low, out_high), row_swap(jnp.where(lower, out_high, out_low))], axis=2
    )

    mine = (r * 8 + c) * OWN_TOKENS
    theirs = ((1 - r) * 8 + c) * OWN_TOKENS
    gains_flat = norm_gains.reshape(4, HALF)
    small = jnp.concatenate(
        [
            lax.dynamic_slice(hidden_in, (theirs, 0), (OWN_TOKENS, HALF)),
            lax.dynamic_slice(cotangent, (theirs, 0), (OWN_TOKENS, HALF)),
            gains_flat,
            jnp.zeros((4, HALF), F32),
        ]
    )
    small = row_swap(small)
    hidden = natural(
        lax.dynamic_slice(hidden_in, (mine, 0), (OWN_TOKENS, HALF)), small[:OWN_TOKENS]
    )
    grad_tokens = natural(
        lax.dynamic_slice(cotangent, (mine, 0), (OWN_TOKENS, HALF)),
        small[OWN_TOKENS : 2 * OWN_TOKENS],
    )
    gains = natural(gains_flat, small[2 * OWN_TOKENS : 2 * OWN_TOKENS + 4])

    k = lax.axis_index("dp")
    others = []
    for layer in range(layers):
        up_sent = lax.dynamic_slice(w_gate_up, (layer, 2 - 2 * r + k // 4, 128 * (k % 4), 0), (1, 1, 128, 2 * FF))
        down_sent = lax.dynamic_slice(w_down, (layer, 2 - 2 * r + k // 4, 128 * (k % 4), 0), (1, 1, 128, HALF))
        piece = row_swap(jnp.concatenate([up_sent[0, 0], down_sent[0, 0]], axis=1))
        others.append(lax.all_gather(piece, "dp", axis=0, tiled=True))
    cot_low = cotangent.astype(BF16)
    upstream = jnp.concatenate([cot_low, row_swap(cot_low)], axis=1)

    router_rows = jnp.transpose(w_router, (0, 2, 1)).reshape(OWN_TOKENS, 256)

    row = jnp.reshape(r, (1,))
    info = jnp.stack([r, 4 * c + 2 * r])
    gain_rows = [gains[i : i + 1] for i in range(4)]
    routers = None
    records = []
    rows_in = normed_first.reshape(PEERS, OWN_TOKENS, MODEL_WIDTH)
    for layer in range(layers):
        partial, *saved = attend(rows_in, heads, out_rows, cosine, sine, layer)
        got = exchange(partial)
        if layer == 0:
            middle, _, send = add_norm(got, hidden, gain_rows[1], router_rows)
            got = exchange(send)
            table = got[:, :, MODEL_WIDTH:].reshape(2, 8, 2, 4, HALF)
            table = jnp.where(lower, table, table[::-1])
            table = jnp.transpose(table, (2, 1, 3, 0, 4)).reshape(2, 32, MODEL_WIDTH)
            routers = [table[0], table[1]]
        else:
            middle, _, send = add_norm(got, hidden, gain_rows[2 * layer + 1])
            got = exchange(send)
        normed_two = got
        partial, pre, gates = experts(
            info, normed_two, routers[layer], expert_ids, w_gate_up, w_down, others[layer], layer
        )
        got = exchange(partial)
        rec = dict(hidden=hidden, normed_one=rows_in, saved=saved, middle=middle)
        rec.update(normed_two=normed_two, gates=gates, pre=pre)
        if layer + 1 < layers:
            hidden, mixed, send = add_norm(got, middle, gain_rows[2 * layer + 2])
            rows_in = exchange(send)
        else:
            mixed, send = add_last(got, middle, grad_tokens)
            got = exchange(send).reshape(TOKENS, HALF + 128)
            block_out = got[:, :HALF].astype(F32)
            mean = got[:, HALF:]
        rec.update(mixed=mixed)
        records.append(rec)

    packs, smalls = [None] * layers, [None] * layers
    gain_sums = [None] * 4
    for layer in reversed(range(layers)):
        rec = records[layer]
        partial, grad_pre, act, grad_y, grad_logits = experts_back(
            info, upstream, mean, rec["gates"], rec["pre"], routers[layer],
            w_gate_up, w_down, others[layer], layer,
        )
        got = exchange(partial)
        pack, router_grad = experts_grads(rec["normed_two"], grad_pre, act, grad_y, grad_logits)
        packs[layer] = lax.psum_scatter(pack, "dp", scatter_dimension=0, tiled=True)
        grad_middle, send = middle_back(got, rec["middle"], gain_rows[2 * layer + 1], grad_tokens)
        low = exchange(send)
        send, smalls[layer], gain_sums[2 * layer + 1] = attend_back(
            row, low, rec["normed_one"], heads, out_rows, cosine, sine, rec["saved"],
            router_grad, gain_rows[2 * layer], layer,
        )
        got = exchange(send)
        if layer > 0:
            grad_tokens, gain_sums[2 * layer], send = first_back(
                got, rec["hidden"], gain_rows[2 * layer], grad_middle, records[layer - 1]["mixed"]
            )
            got = exchange(send)
            upstream = got[:, :, :MODEL_WIDTH].reshape(TOKENS, MODEL_WIDTH)
            mean = got[:, :, MODEL_WIDTH:].reshape(TOKENS, 128)
        else:
            _, gain_sums[0], send = first_back(got, rec["hidden"], gain_rows[0], grad_middle)
            grad_hidden = exchange(send).reshape(TOKENS, HALF).astype(F32)

    gain_flat = jnp.concatenate([g[:8] + g[8:] for g in gain_sums], axis=1)
    high, low = split_two(gain_flat)
    gain_block = jnp.broadcast_to(jnp.concatenate([high, low])[None], (N_DP, 16, 512))
    smalls[0] = lax.dynamic_update_slice(smalls[0], gain_block, (0, 128, 0))

    grads = []
    for layer in range(layers):
        if layer == 0:
            got = lax.all_to_all(smalls[layer], "dp", 0, 0, tiled=True).astype(F32)
            mine_small = jnp.sum(got, axis=0)
            flat = (mine_small[128:136] + mine_small[136:]).reshape(8, 4, 128)
            flat = lax.dynamic_index_in_dim(flat, 4 * r + k // 2, 0, keepdims=False)
            flat = flat.reshape(4, 2, 64)
            gain_out = lax.dynamic_index_in_dim(flat, k % 2, 1, keepdims=False).reshape(2, 2, 64)
        else:
            mine_small = lax.psum_scatter(smalls[layer], "dp", scatter_dimension=0, tiled=True)
            mine_small = mine_small[0].astype(F32)
        big = packs[layer][0]
        total = mine_small[:64] + row_swap(mine_small[64:128].astype(BF16)).astype(F32)
        grad_qkv = total[:, :256]
        grad_out = total[:, 256:384].reshape(4, 16, 128).transpose(1, 0, 2).reshape(16, HALF)
        grad_router = lax.dynamic_slice(total, (0, 384 + 4 * c), (64, 4))
        big = big.reshape(2, 192, MODEL_WIDTH)
        up_pieces = big[:, :128].reshape(2, 2, 64, MODEL_WIDTH)
        down_pieces = big[:, 128:]
        up_other = row_swap(up_pieces[:, 1])
        down_other = row_swap(down_pieces[:, :, HALF:])
        up_mine, down_mine = up_pieces[:, 0], down_pieces[:, :, :HALF]
        grad_up = jnp.where(
            lower,
            jnp.concatenate([up_mine, up_other]),
            jnp.concatenate([up_other, up_mine]),
        ).astype(F32)
        grad_down = jnp.where(
            lower,
            jnp.concatenate([down_mine, down_other]),
            jnp.concatenate([down_other, down_mine]),
        ).astype(F32)
        grads.append((grad_qkv, grad_out, grad_router, grad_up, grad_down))
    return (block_out, grad_hidden, gain_out) + tuple(
        jnp.stack([grads[layer][i] for layer in range(layers)]) for i in range(5)
    )


def solution(mesh):
    placed = (
        P("dp", "row"),
        P("dp", "row"),
        P(None, None, "row"),
        P(None, "row", "col"),
        P(None, "col", "row"),
        P(None, "row", "col"),
        P(None, "col", "row", None),
        P(None, "col", None, "row"),
        P(None, "dp", None),
    )
    return jax.shard_map(
        body,
        mesh=mesh,
        in_specs=placed,
        out_specs=(
            P("dp", "row"),
            P("dp", "row"),
            P(None, None, ("row", "dp")),
            P(None, ("row", "dp"), "col"),
            P(None, ("col", "dp"), "row"),
            P(None, ("row", "dp"), "col"),
            P(None, "col", ("row", "dp"), None),
            P(None, "col", "dp", "row"),
        ),
        check_vma=False,
    )
```

profile of v0, /device:TPU:0, one launch (start us, length us, event | category | flops | bytes accessed | tf_op | source)
XLA Modules:
  0.0 431.3 jit_solution(3219592453653909196)
XLA Ops:
  9.5 2.1 collective-permute-start.4
  11.6 9.1 %collective-permute-done.4 = bf16[128,1536]{1,0:T(8,128)(2,1)S(1)} collective-permute-done((bf16[128,1536]{1,0:T(8,128)(2,1)S(1)}, bf16[128,1536]{1,0:T(8,128)(2,1)S(1)}, u32[]{:S(2)}, u32[]{:S(2)}) %collective-permute-start.4) | collective-permute-done | bytes 393248 | tf_op jit(solution)/shard_map/ppermute | solution.py:40
  23.6 1.7 collective-permute-start.3
  25.7 1.8 collective-permute-start.5
  28.1 10.7 %collective-permute-done.5 = bf16[128,1536]{1,0:T(8,128)(2,1)S(1)} collective-permute-done((bf16[128,1536]{1,0:T(8,128)(2,1)S(1)}, bf16[128,1536]{1,0:T(8,128)(2,1)S(1)}, u32[]{:S(2)}, u32[]{:S(2)}) %collective-permute-start.5) | collective-permute-done | bytes 393248 | tf_op jit(solution)/shard_map/ppermute | solution.py:40
  40.5 1.2 collective-permute-start
  43.0 1.3 reshape.390.rest_0_
  46.8 4.7 %collective-permute-done = bf16[256,640]{0,1:T(8,128)(2,1)} collective-permute-done((bf16[256,640]{0,1:T(8,128)(2,1)}, bf16[256,640]{0,1:T(8,128)(2,1)}, u32[]{:S(2)}, u32[]{:S(2)}) %collective-permute-start) | collective-permute-done | bytes 327712 | tf_op jit(solution)/shard_map/ppermute | solution.py:40
  54.4 5.8 %collective-permute-done.1 = bf16[2,512,192]{2,1,0:T(8,128)(2,1)S(1)} collective-permute-done((bf16[2,512,192]{2,1,0:T(8,128)(2,1)S(1)}, bf16[2,512,192]{2,1,0:T(8,128)(2,1)S(1)}, u32[]{:S(2)}, u32[]{:S(2)}) %collective-permute-start.1) | collective-permute-done | bytes 393248 | tf_op jit(solution)/shard_map/ppermute | solution.py:40
  60.3 1.3 pad_maximum_fusion.heads_ref
  61.5 3.4 attend.2
  65.0 7.5 %all-to-all-start = ((bf16[16,16,1024]{2,1,0:T(8,128)(2,1)}), bf16[16,16,1024]{2,1,0:T(8,128)(2,1)S(1)}, u32[]{:S(2)}, u32[]{:S(2)}) async-start(bf16[16,16,1024]{2,1,0:T(8,128)(2,1)} %get-tuple-element.59), calls=%async_computation | async-start | bytes 1048576 | tf_op jit(solution)/shard_map/all_to_all | solution.py:593
  75.2 7.3 %all-to-all-done.got_ref = bf16[16,16,1024]{2,1,0:T(8,128)(2,1)S(1)} async-done(((bf16[16,16,1024]{2,1,0:T(8,128)(2,1)}), bf16[16,16,1024]{2,1,0:T(8,128)(2,1)S(1)}, u32[]{:S(2)}, u32[]{:S(2)}) %all-to-all-start) | async-done | bytes 524320 | tf_op jit(solution)/shard_map/all_to_all | solution.py:593
  83.3 2.1 add_norm.3
  85.4 3.6 all-to-all-start.1
  90.5 9.2 %all-to-all-done.1.x_ref = bf16[16,16,1280]{2,1,0:T(8,128)(2,1)S(1)} async-done(((bf16[16,16,1280]{2,1,0:T(8,128)(2,1)}), bf16[16,16,1280]{2,1,0:T(8,128)(2,1)S(1)}, u32[]{:S(2)}, u32[]{:S(2)}) %all-to-all-start.1) | async-done | bytes 655392 | tf_op jit(solution)/shard_map/all_to_all | solution.py:593
  100.6 7.1 %experts.2 = (bf16[16,16,1024]{2,1,0:T(8,128)(2,1)}, f32[2,256,1024]{2,1,0:T(8,128)}, f32[256,32]{1,0:T(8,128)}) custom-call(s32[2]{0:T(128)} %pad_add_fusion.info_ref, bf16[16,16,1280]{2,1,0:T(8,128)(2,1)} %copy-done, bf16[32,1024]{1,0:T(8,128)(2,1)} %bitcast.94, s32[2,256,8]{2,1,0:T(8,128)} %copy.34.ids_ref, bf16[2,4,512,1024]{3,2,1,0:T(8,128)(2,1)} %up_ref.7, ...), custom_call_target="tpu_custom_call" | custom-call | flops 1600000000 | bytes 9000000 | tf_op jit(solution)/shard_map/experts/pallas_call | solution.py:298
  107.7 14.2 %all_to_all.85.got_ref = bf16[16,16,1024]{2,1,0:T(8,128)(2,1)} all-to-all(bf16[16,16,1024]{2,1,0:T(8,128)(2,1)} %get-tuple-element.61), channel_id=1, replica_groups=mesh['dp'=8,'row'=2,'col'=8] {'row','col'}, dimensions={0} | all-to-all | bytes 1048576 | tf_op jit(solution)/shard_map/all_to_all | solution.py:593
  121.9 2.1 add_norm.4
  124.0 14.2 %all_to_all.86.x_ref = bf16[16,16,1024]{2,1,0:T(8,128)(2,1)} all-to-all(bf16[16,16,1024]{2,1,0:T(8,128)(2,1)} %get-tuple-element.63), channel_id=1, replica_groups=mesh['dp'=8,'row'=2,'col'=8] {'row','col'}, dimensions={0} | all-to-all | bytes 1048576 | tf_op jit(solution)/shard_map/all_to_all | solution.py:593
  138.2 3.3 attend.3
  141.6 14.2 %all_to_all.87.got_ref = bf16[16,16,1024]{2,1,0:T(8,128)(2,1)} all-to-all(bf16[16,16,1024]{2,1,0:T(8,128)(2,1)} %get-tuple-element.64), channel_id=1, replica_groups=mesh['dp'=8,'row'=2,'col'=8] {'row','col'}, dimensions={0} | all-to-all | bytes 1048576 | tf_op jit(solution)/shard_map/all_to_all | solution.py:593
  155.8 2.1 add_norm.5
  157.8 3.6 all-to-all-start.5
  162.1 9.3 %all-to-all-done.5.x_ref = bf16[16,16,1024]{2,1,0:T(8,128)(2,1)S(1)} async-done(((bf16[16,16,1024]{2,1,0:T(8,128)(2,1)}), bf16[16,16,1024]{2,1,0:T(8,128)(2,1)S(1)}, u32[]{:S(2)}, u32[]{:S(2)}) %all-to-all-start.5) | async-done | bytes 524320 | tf_op jit(solution)/shard_map/all_to_all | solution.py:593
  172.2 7.2 %experts.3 = (bf16[16,16,1024]{2,1,0:T(8,128)(2,1)}, f32[2,256,1024]{2,1,0:T(8,128)}, f32[256,32]{1,0:T(8,128)}) custom-call(s32[2]{0:T(128)} %pad_add_fusion.info_ref, bf16[16,16,1024]{2,1,0:T(8,128)(2,1)} %copy-done.5, bf16[32,1024]{1,0:T(8,128)(2,1)} %bitcast.96, s32[2,256,8]{2,1,0:T(8,128)} %copy.34.ids_ref, bf16[2,4,512,1024]{3,2,1,0:T(8,128)(2,1)} %up_ref.7, ...), custom_call_target="tpu_custom_call" | custom-call | flops 1600000000 | bytes 9000000 | tf_op jit(solution)/shard_map/experts/pallas_call | solution.py:298
  179.5 3.6 all-to-all-start.6
  183.1 2.1 collective-permute-start.6
  185.9 7.3 %all-to-all-done.6.got_ref = bf16[16,16,1024]{2,1,0:T(8,128)(2,1)S(1)} async-done(((bf16[16,16,1024]{2,1,0:T(8,128)(2,1)}), bf16[16,16,1024]{2,1,0:T(8,128)(2,1)S(1)}, u32[]{:S(2)}, u32[]{:S(2)}) %all-to-all-start.6) | async-done | bytes 524320 | tf_op jit(solution)/shard_map/all_to_all | solution.py:593
  193.9 2.0 add_last.1
  195.9 3.6 all-to-all-start.7
  200.3 8.2 %all-to-all-done.7 = bf16[16,16,640]{2,1,0:T(8,128)(2,1)S(1)} async-done(((bf16[16,16,640]{2,1,0:T(8,128)(2,1)}), bf16[16,16,640]{2,1,0:T(8,128)(2,1)S(1)}, u32[]{:S(2)}, u32[]{:S(2)}) %all-to-all-start.7) | async-done | bytes 327712 | tf_op jit(solution)/shard_map/all_to_all | solution.py:593
  209.2 8.1 %experts_back.2 = (bf16[16,16,1024]{2,1,0:T(8,128)(2,1)}, bf16[2,256,1024]{2,1,0:T(8,128)(2,1)}, bf16[2,256,512]{2,1,0:T(8,128)(2,1)}, bf16[2,256,1024]{2,1,0:T(8,128)(2,1)}, f32[256,32]{1,0:T(8,128)}) custom-call(s32[2]{0:T(128)} %pad_add_fusion.info_ref, bf16[256,1024]{1,0:T(8,128)(2,1)} %pad_maximum_fusion.3.g_ref, bf16[256,128]{1,0:T(8,128)(2,1)} %slice.237.mean_ref, ...), custom_call_target="tpu_custom_call" | custom-call | flops 1700000000 | bytes 11000000 | tf_op jit(solution)/shard_map/experts_back/pallas_call | solution.py:375
  217.3 15.0 %all_to_all.88.got_ref = bf16[16,16,1024]{2,1,0:T(8,128)(2,1)} all-to-all(bf16[16,16,1024]{2,1,0:T(8,128)(2,1)} %get-tuple-element.72), channel_id=1, replica_groups=mesh['dp'=8,'row'=2,'col'=8] {'row','col'}, dimensions={0} | all-to-all | bytes 1048576 | tf_op jit(solution)/shard_map/all_to_all | solution.py:593
  232.3 2.2 middle_back.2
  234.5 4.6 %all-to-all-start.9 = ((bf16[16,16,1152]{2,1,0:T(8,128)(2,1)}), bf16[16,16,1152]{2,1,0:T(8,128)(2,1)S(1)}, u32[]{:S(2)}, u32[]{:S(2)}) async-start(bf16[16,16,1152]{2,1,0:T(8,128)(2,1)} %get-tuple-element.73), calls=%async_computation.9 | async-start | bytes 1179648 | tf_op jit(solution)/shard_map/all_to_all | solution.py:593
  239.2 5.8 %experts_grads.2 = (bf16[8,384,1024]{2,1,0:T(8,128)(2,1)}, f32[1024,32]{1,0:T(8,128)}) custom-call(bf16[16,16,1024]{2,1,0:T(8,128)(2,1)} %copy-done.5, bf16[2,256,1024]{2,1,0:T(8,128)(2,1)} %get-tuple-element.77.grad_pre_ref, bf16[2,256,512]{2,1,0:T(8,128)(2,1)} %get-tuple-element.78.act_ref, bf16[2,256,1024]{2,1,0:T(8,128)(2,1)} %get-tuple-element.79.grad_y_ref, ...), custom_call_target="tpu_custom_call" | custom-call | flops 1600000000 | bytes 9000000 | tf_op jit(solution)/shard_map/experts_grads/pallas_call | solution.py:427
  245.0 4.7 %all-to-all-done.9.low_ref = bf16[16,16,1152]{2,1,0:T(8,128)(2,1)S(1)} async-done(((bf16[16,16,1152]{2,1,0:T(8,128)(2,1)}), bf16[16,16,1152]{2,1,0:T(8,128)(2,1)S(1)}, u32[]{:S(2)}, u32[]{:S(2)}) %all-to-all-start.9) | async-done | bytes 589856 | tf_op jit(solution)/shard_map/all_to_all | solution.py:593
  250.5 5.3 %attend_back.2 = (bf16[16,16,1152]{2,1,0:T(8,128)(2,1)}, bf16[8,144,512]{2,1,0:T(8,128)(2,1)}, f32[16,128]{1,0:T(8,128)}) custom-call(s32[1]{0:T(128)} %bitcast.row_ref, bf16[16,16,1152]{2,1,0:T(8,128)(2,1)} %copy-done.4, bf16[16,16,1024]{2,1,0:T(8,128)(2,1)} %all_to_all.86.x_ref, bf16[2,1024,192]{2,1,0:T(8,128)(2,1)} %pad_maximum_fusion.heads_ref, ...), custom_call_target="tpu_custom_call" | custom-call | flops 500000000 | bytes 4000000 | tf_op jit(solution)/shard_map/attend_back/pallas_call | solution.py:214
  256.9 16.2 %all_to_all.89.got_ref = bf16[16,16,1152]{2,1,0:T(8,128)(2,1)} all-to-all(bf16[16,16,1152]{2,1,0:T(8,128)(2,1)S(1)} %copy-done.10), channel_id=1, replica_groups=mesh['dp'=8,'row'=2,'col'=8] {'row','col'}, dimensions={0} | all-to-all | bytes 1179648 | tf_op jit(solution)/shard_map/all_to_all | solution.py:593
  273.1 2.2 first_back.2
  275.4 14.2 %all_to_all.90 = bf16[16,16,1152]{2,1,0:T(8,128)(2,1)S(1)} all-to-all(bf16[16,16,1152]{2,1,0:T(8,128)(2,1)} %get-tuple-element.85), channel_id=1, replica_groups=mesh['dp'=8,'row'=2,'col'=8] {'row','col'}, dimensions={0} | all-to-all | bytes 1179648 | tf_op jit(solution)/shard_map/all_to_all | solution.py:593
  291.0 8.0 %experts_back.3 = (bf16[16,16,1024]{2,1,0:T(8,128)(2,1)}, bf16[2,256,1024]{2,1,0:T(8,128)(2,1)}, bf16[2,256,512]{2,1,0:T(8,128)(2,1)}, bf16[2,256,1024]{2,1,0:T(8,128)(2,1)}, f32[256,32]{1,0:T(8,128)}) custom-call(s32[2]{0:T(128)} %pad_add_fusion.info_ref, bf16[256,1024]{1,0:T(8,128)(2,1)} %bitcast.83, bf16[256,128]{1,0:T(8,128)(2,1)} %bitcast.100, ...), custom_call_target="tpu_custom_call" | custom-call | flops 1700000000 | bytes 11000000 | tf_op jit(solution)/shard_map/experts_back/pallas_call | solution.py:375
  299.0 5.8 %experts_grads.3 = (bf16[8,384,1024]{2,1,0:T(8,128)(2,1)}, f32[1024,32]{1,0:T(8,128)}) custom-call(bf16[16,16,1280]{2,1,0:T(8,128)(2,1)} %copy-done, bf16[2,256,1024]{2,1,0:T(8,128)(2,1)} %get-tuple-element.94.grad_pre_ref, bf16[2,256,512]{2,1,0:T(8,128)(2,1)} %get-tuple-element.95.act_ref, bf16[2,256,1024]{2,1,0:T(8,128)(2,1)} %get-tuple-element.96.grad_y_ref, ...), custom_call_target="tpu_custom_call" | custom-call | flops 1600000000 | bytes 9000000 | tf_op jit(solution)/shard_map/experts_grads/pallas_call | solution.py:427
  305.8 13.5 %all_to_all.91.got_ref = bf16[16,16,1024]{2,1,0:T(8,128)(2,1)} all-to-all(bf16[16,16,1024]{2,1,0:T(8,128)(2,1)S(1)} %copy-done.11), channel_id=1, replica_groups=mesh['dp'=8,'row'=2,'col'=8] {'row','col'}, dimensions={0} | all-to-all | bytes 1048576 | tf_op jit(solution)/shard_map/all_to_all | solution.py:593
  319.3 2.1 middle_back.3
  321.5 3.8 all-to-all-start.13
  325.3 13.3 %all-to-all-done.13.low_ref = bf16[16,16,1152]{2,1,0:T(8,128)(2,1)S(1)} async-done(((bf16[16,16,1152]{2,1,0:T(8,128)(2,1)}), bf16[16,16,1152]{2,1,0:T(8,128)(2,1)S(1)}, u32[]{:S(2)}, u32[]{:S(2)}) %all-to-all-start.13) | async-done | bytes 589856 | tf_op jit(solution)/shard_map/all_to_all | solution.py:593
  339.5 5.8 %attend_back.3 = (bf16[16,16,1152]{2,1,0:T(8,128)(2,1)}, bf16[8,144,512]{2,1,0:T(8,128)(2,1)}, f32[16,128]{1,0:T(8,128)}) custom-call(s32[1]{0:T(128)} %bitcast.row_ref, bf16[16,16,1152]{2,1,0:T(8,128)(2,1)} %copy-done.3, bf16[16,16,1024]{2,1,0:T(8,128)(2,1)} %pad_maximum_fusion.1.x_ref, bf16[2,1024,192]{2,1,0:T(8,128)(2,1)} %pad_maximum_fusion.heads_ref, ...), custom_call_target="tpu_custom_call" | custom-call | flops 500000000 | bytes 4000000 | tf_op jit(solution)/shard_map/attend_back/pallas_call | solution.py:214
  345.3 3.6 all-to-all-start.14
  349.6 9.6 %all-to-all-done.14.got_ref = bf16[16,16,1152]{2,1,0:T(8,128)(2,1)S(1)} async-done(((bf16[16,16,1152]{2,1,0:T(8,128)(2,1)}), bf16[16,16,1152]{2,1,0:T(8,128)(2,1)S(1)}, u32[]{:S(2)}, u32[]{:S(2)}) %all-to-all-start.14) | async-done | bytes 589856 | tf_op jit(solution)/shard_map/all_to_all | solution.py:593
  360.0 2.0 first_back.3
  362.0 3.6 all-to-all-start.15
  367.0 7.4 %all-to-all-done.15 = bf16[16,16,512]{2,1,0:T(8,128)(2,1)S(1)} async-done(((bf16[16,16,512]{2,1,0:T(8,128)(2,1)}), bf16[16,16,512]{2,1,0:T(8,128)(2,1)S(1)}, u32[]{:S(2)}, u32[]{:S(2)}) %all-to-all-start.15) | async-done | bytes 262176 | tf_op jit(solution)/shard_map/all_to_all | solution.py:593
  374.4 4.6 %all-to-all-start.16 = ((bf16[8,144,512]{2,1,0:T(8,128)(2,1)}), bf16[8,144,512]{2,1,0:T(8,128)(2,1)S(1)}, u32[]{:S(2)}, u32[]{:S(2)}) async-start(bf16[8,144,512]{2,1,0:T(8,128)(2,1)} %broadcast_dynamic-update-slice_fusion), calls=%async_computation.16 | async-start | bytes 2359296 | tf_op jit(solution)/shard_map/all_to_all | solution.py:758
  381.3 3.1 collective-permute-done.8
  386.1 10.2 %all-to-all-done.16 = bf16[8,144,512]{2,1,0:T(8,128)(2,1)S(1)} async-done(((bf16[8,144,512]{2,1,0:T(8,128)(2,1)}), bf16[8,144,512]{2,1,0:T(8,128)(2,1)S(1)}, u32[]{:S(2)}, u32[]{:S(2)}) %all-to-all-start.16) | async-done | bytes 1179680 | tf_op jit(solution)/shard_map/all_to_all | solution.py:758
  397.8 3.1 collective-permute-done.7
  405.9 1.5 collective-permute-start.10
  407.5 4.3 collective-permute-done.12
  414.6 1.5 collective-permute-start.9
  417.2 3.2 collective-permute-done.11
  421.5 1.8 collective-permute-done.9
  423.3 1.5 maximum_convert_fusion
  (165 shorter events, 48.5 us)
Async XLA Ops:
  7.2 14.3 %copy-start.18 = (f32[2,2,512]{2,1,0:T(2,128)S(1)}, f32[2,2,512]{2,1,0:T(2,128)}, u32[]{:S(2)}) copy-start(f32[2,2,512]{2,1,0:T(2,128)} %param.11) | copy-start | bytes 24580
  7.2 14.5 %copy-start.9 = (f32[256,512]{1,0:T(8,128)S(1)}, f32[256,512]{1,0:T(8,128)}, u32[]{:S(2)}) copy-start(f32[256,512]{1,0:T(8,128)} %param.10) | copy-start | bytes 1572868
  7.2 15.1 %copy-start.1 = (f32[256,512]{1,0:T(8,128)S(1)}, f32[256,512]{1,0:T(8,128)}, u32[]{:S(2)}) copy-start(f32[256,512]{1,0:T(8,128)} %param.9) | copy-start | bytes 1572868
  7.2 18.1 %copy-start.14 = (bf16[2,128,512]{2,1,0:T(8,128)(2,1)S(1)}, bf16[2,128,512]{2,1,0:T(8,128)(2,1)}, u32[]{:S(2)}) copy-start(bf16[2,128,512]{2,1,0:T(8,128)(2,1)} %param.13) | copy-start | bytes 786436
  7.2 93.4 %all-gather.3.cloned.1.call-start = ((), (), s32[]{:S(2)}) async-start(), calls=%async_computation.20 | async-start | bytes 3538944 | tf_op jit(solution)/shard_map/all_gather | solution.py:678
  9.5 11.2 %collective-permute-start.4 = (bf16[128,1536]{1,0:T(8,128)(2,1)S(1)}, bf16[128,1536]{1,0:T(8,128)(2,1)S(1)}, u32[]{:S(2)}, u32[]{:S(2)}) collective-permute-start(bf16[128,1536]{1,0:T(8,128)(2,1)S(1)} %pad_maximum_fusion.4), channel_id=1, source_target_pairs={{0,8},{8,0},{1,9},{9,1},{2,10},{10,2},{3,11},{11,3},{4,12},{12,4},... | collective-permute-start | bytes 1179656 | tf_op jit(solution)/shard_map/ppermute | solution.py:40
  20.7 0.8 copy-start.12
  21.5 140.7 %all-gather.5.cloned.1.call-start = ((), (), s32[]{:S(2)}) async-start(), calls=%async_computation.21 | async-start | bytes 3538944 | tf_op jit(solution)/shard_map/all_gather | solution.py:678
  23.6 48.9 %collective-permute-start.3 = (f32[40,512]{1,0:T(8,128)}, f32[40,512]{1,0:T(8,128)}, u32[]{:S(2)}, u32[]{:S(2)}) collective-permute-start(f32[40,512]{1,0:T(8,128)} %maximum_maximum_fusion.1), channel_id=1, source_target_pairs={{0,8},{8,0},{1,9},{9,1},{2,10},{10,2},{3,11},{11,3},{4,12},{12,4},... | collective-permute-start | bytes 245768 | tf_op jit(solution)/shard_map/ppermute | solution.py:40
  25.3 16.4 %copy-start.8 = (bf16[2,512,256]{2,1,0:T(8,128)(2,1)S(1)}, bf16[2,512,256]{2,1,0:T(8,128)(2,1)}, u32[]{:S(2)}) copy-start(bf16[2,512,256]{2,1,0:T(8,128)(2,1)} %param.12) | copy-start | bytes 1572868
  25.3 20.7 %collective-permute-start.2 = (bf16[2,64,512]{2,1,0:T(8,128)(2,1)S(1)}, bf16[2,64,512]{2,1,0:T(8,128)(2,1)S(1)}, u32[]{:S(2)}, u32[]{:S(2)}) collective-permute-start(bf16[2,64,512]{2,1,0:T(8,128)(2,1)S(1)} %get-tuple-element.129), channel_id=1, source_target_pairs={{0,8},{8,0},{1,9},{9,1},{2,10},{10,2},{3,11},{11,3},{4,12},{12,4},... | collective-permute-start | bytes 393224 | tf_op jit(solution)/shard_map/ppermute | solution.py:40
  25.7 13.1 %collective-permute-start.5 = (bf16[128,1536]{1,0:T(8,128)(2,1)S(1)}, bf16[128,1536]{1,0:T(8,128)(2,1)S(1)}, u32[]{:S(2)}, u32[]{:S(2)}) collective-permute-start(bf16[128,1536]{1,0:T(8,128)(2,1)S(1)} %pad_maximum_fusion.5), channel_id=1, source_target_pairs={{0,8},{8,0},{1,9},{9,1},{2,10},{10,2},{3,11},{11,3},{4,12},{12,4},... | collective-permute-start | bytes 1179656 | tf_op jit(solution)/shard_map/ppermute | solution.py:40
  38.8 0.7 copy-start.13
  40.5 11.0 %collective-permute-start = (bf16[256,640]{0,1:T(8,128)(2,1)}, bf16[256,640]{0,1:T(8,128)(2,1)}, u32[]{:S(2)}, u32[]{:S(2)}) collective-permute-start(bf16[256,640]{0,1:T(8,128)(2,1)} %maximum_maximum_fusion), channel_id=1, source_target_pairs={{0,8},{8,0},{1,9},{9,1},{2,10},{10,2},{3,11},{11,3},{4,12},{12,4},... | collective-permute-start | bytes 983048 | tf_op jit(solution)/shard_map/ppermute | solution.py:40
  42.1 18.2 %collective-permute-start.1 = (bf16[2,512,192]{2,1,0:T(8,128)(2,1)S(1)}, bf16[2,512,192]{2,1,0:T(8,128)(2,1)S(1)}, u32[]{:S(2)}, u32[]{:S(2)}) collective-permute-start(bf16[2,512,192]{2,1,0:T(8,128)(2,1)S(1)} %pad_maximum_fusion.2), channel_id=1, source_target_pairs={{0,8},{8,0},{1,9},{9,1},{2,10},{10,2},{3,11},{11,3},{4,12},{12,4},... | collective-permute-start | bytes 1179656 | tf_op jit(solution)/shard_map/ppermute | solution.py:40
  61.5 12.4 %copy-start.16 = (f32[16,512]{1,0:T(8,128)S(1)}, f32[16,512]{1,0:T(8,128)}, u32[]{:S(2)}) copy-start(f32[16,512]{1,0:T(8,128)} %get-tuple-element.124) | copy-start | bytes 98308
  65.0 24.0 %copy-start.17 = (s32[2,256,8]{1,2,0:T(8,128)S(1)}, s32[2,256,8]{1,2,0:T(8,128)}, u32[]{:S(2)}) copy-start(s32[2,256,8]{1,2,0:T(8,128)} %param.17) | copy-start | bytes 49156
  65.0 17.5 %all-to-all-start = ((bf16[16,16,1024]{2,1,0:T(8,128)(2,1)}), bf16[16,16,1024]{2,1,0:T(8,128)(2,1)S(1)}, u32[]{:S(2)}, u32[]{:S(2)}) async-start(bf16[16,16,1024]{2,1,0:T(8,128)(2,1)} %get-tuple-element.59), calls=%async_computation | async-start | bytes 1048576 | tf_op jit(solution)/shard_map/all_to_all | solution.py:593
  82.5 0.8 copy-start.7
  85.4 14.3 %all-to-all-start.1 = ((bf16[16,16,1280]{2,1,0:T(8,128)(2,1)}), bf16[16,16,1280]{2,1,0:T(8,128)(2,1)S(1)}, u32[]{:S(2)}, u32[]{:S(2)}) async-start(bf16[16,16,1280]{2,1,0:T(8,128)(2,1)} %get-tuple-element.60), calls=%async_computation.1 | async-start | bytes 1310720 | tf_op jit(solution)/shard_map/all_to_all | solution.py:593
  99.7 0.9 copy-start
  157.8 13.6 %all-to-all-start.5 = ((bf16[16,16,1024]{2,1,0:T(8,128)(2,1)}), bf16[16,16,1024]{2,1,0:T(8,128)(2,1)S(1)}, u32[]{:S(2)}, u32[]{:S(2)}) async-start(bf16[16,16,1024]{2,1,0:T(8,128)(2,1)} %get-tuple-element.66), calls=%async_computation.5 | async-start | bytes 1048576 | tf_op jit(solution)/shard_map/all_to_all | solution.py:593
  171.5 0.8 copy-start.5
  172.2 13.0 %copy-start.15 = (f32[16,512]{1,0:T(8,128)S(1)}, f32[16,512]{1,0:T(8,128)}, u32[]{:S(2)}) copy-start(f32[16,512]{1,0:T(8,128)} %get-tuple-element.122) | copy-start | bytes 98308
  179.5 13.6 %all-to-all-start.6 = ((bf16[16,16,1024]{2,1,0:T(8,128)(2,1)}), bf16[16,16,1024]{2,1,0:T(8,128)(2,1)S(1)}, u32[]{:S(2)}, u32[]{:S(2)}) async-start(bf16[16,16,1024]{2,1,0:T(8,128)(2,1)} %get-tuple-element.67), calls=%async_computation.6 | async-start | bytes 1048576 | tf_op jit(solution)/shard_map/all_to_all | solution.py:593
  183.1 16.4 %collective-permute-start.6 = (bf16[256,512]{1,0:T(8,128)(2,1)S(1)}, bf16[256,512]{1,0:T(8,128)(2,1)S(1)}, u32[]{:S(2)}, u32[]{:S(2)}) collective-permute-start(bf16[256,512]{1,0:T(8,128)(2,1)S(1)} %convert_element_type.109), channel_id=1, source_target_pairs={{0,8},{8,0},{1,9},{9,1},{2,10},{10,2},{3,11},{11,3},{4,12},{12,4},... | collective-permute-start | bytes 786440 | tf_op jit(solution)/shard_map/ppermute | solution.py:40
  193.1 0.8 copy-start.6
  195.9 12.7 %all-to-all-start.7 = ((bf16[16,16,640]{2,1,0:T(8,128)(2,1)}), bf16[16,16,640]{2,1,0:T(8,128)(2,1)S(1)}, u32[]{:S(2)}, u32[]{:S(2)}) async-start(bf16[16,16,640]{2,1,0:T(8,128)(2,1)} %get-tuple-element.69), calls=%async_computation.7 | async-start | bytes 655360 | tf_op jit(solution)/shard_map/all_to_all | solution.py:593
  234.5 15.2 %all-to-all-start.9 = ((bf16[16,16,1152]{2,1,0:T(8,128)(2,1)}), bf16[16,16,1152]{2,1,0:T(8,128)(2,1)S(1)}, u32[]{:S(2)}, u32[]{:S(2)}) async-start(bf16[16,16,1152]{2,1,0:T(8,128)(2,1)} %get-tuple-element.73), calls=%async_computation.9 | async-start | bytes 1179648 | tf_op jit(solution)/shard_map/all_to_all | solution.py:593
  239.1 139.8 %reduce-scatter.4.cloned.1.call-start = ((), (), s32[]{:S(2)}) async-start(), calls=%async_computation.22 | async-start | bytes 1327104 | tf_op jit(solution)/shard_map/reduce_scatter | solution.py:765
  249.7 0.8 copy-start.4
  255.8 147.4 %reduce-scatter.8.cloned.1.call-start = ((), (), s32[]{:S(2)}) async-start(), calls=%async_computation.24 | async-start | bytes 7077888 | tf_op jit(solution)/shard_map/reduce_scatter | solution.py:731
  255.8 1.1 copy-start.10
  256.4 155.5 %reduce-scatter.6.cloned.1.call-start = ((), (), s32[]{:S(2)}) async-start(), calls=%async_computation.23 | async-start | bytes 7077888 | tf_op jit(solution)/shard_map/reduce_scatter | solution.py:731
  304.7 1.1 copy-start.11
  321.5 17.2 %all-to-all-start.13 = ((bf16[16,16,1152]{2,1,0:T(8,128)(2,1)}), bf16[16,16,1152]{2,1,0:T(8,128)(2,1)S(1)}, u32[]{:S(2)}, u32[]{:S(2)}) async-start(bf16[16,16,1152]{2,1,0:T(8,128)(2,1)} %get-tuple-element.90), calls=%async_computation.13 | async-start | bytes 1179648 | tf_op jit(solution)/shard_map/all_to_all | solution.py:593
  338.6 0.8 copy-start.3
  339.4 9.4 %copy-start.19 = (f32[16,128]{1,0:T(8,128)S(1)}, f32[16,128]{1,0:T(8,128)}, u32[]{:S(2)}) copy-start(f32[16,128]{1,0:T(8,128)} %get-tuple-element.106) | copy-start | bytes 24580
  339.4 9.4 %copy-start.20 = (f32[16,128]{1,0:T(8,128)S(1)}, f32[16,128]{1,0:T(8,128)}, u32[]{:S(2)}) copy-start(f32[16,128]{1,0:T(8,128)} %get-tuple-element.105) | copy-start | bytes 24580
  345.3 13.9 %all-to-all-start.14 = ((bf16[16,16,1152]{2,1,0:T(8,128)(2,1)}), bf16[16,16,1152]{2,1,0:T(8,128)(2,1)S(1)}, u32[]{:S(2)}, u32[]{:S(2)}) async-start(bf16[16,16,1152]{2,1,0:T(8,128)(2,1)} %get-tuple-element.99), calls=%async_computation.14 | async-start | bytes 1179648 | tf_op jit(solution)/shard_map/all_to_all | solution.py:593
  359.2 0.8 copy-start.2
  362.0 12.4 %all-to-all-start.15 = ((bf16[16,16,512]{2,1,0:T(8,128)(2,1)}), bf16[16,16,512]{2,1,0:T(8,128)(2,1)S(1)}, u32[]{:S(2)}, u32[]{:S(2)}) async-start(bf16[16,16,512]{2,1,0:T(8,128)(2,1)} %get-tuple-element.101), calls=%async_computation.15 | async-start | bytes 524288 | tf_op jit(solution)/shard_map/all_to_all | solution.py:593
  374.4 22.0 %all-to-all-start.16 = ((bf16[8,144,512]{2,1,0:T(8,128)(2,1)}), bf16[8,144,512]{2,1,0:T(8,128)(2,1)S(1)}, u32[]{:S(2)}, u32[]{:S(2)}) async-start(bf16[8,144,512]{2,1,0:T(8,128)(2,1)} %broadcast_dynamic-update-slice_fusion), calls=%async_computation.16 | async-start | bytes 2359296 | tf_op jit(solution)/shard_map/all_to_all | solution.py:758
  379.8 4.5 %collective-permute-start.8 = (bf16[64,512]{1,0:T(8,128)(2,1)S(1)}, bf16[64,512]{1,0:T(8,128)(2,1)S(1)}, u32[]{:S(2)}, u32[]{:S(2)}) collective-permute-start(bf16[64,512]{1,0:T(8,128)(2,1)S(1)} %slice_bitcast_fusion.7), channel_id=1, source_target_pairs={{0,8},{8,0},{1,9},{9,1},{2,10},{10,2},{3,11},{11,3},{4,12},{12,4},... | collective-permute-start | bytes 196616 | tf_op jit(solution)/shard_map/ppermute | solution.py:40
  396.6 4.3 collective-permute-start.7
  405.2 6.5 %collective-permute-start.12 = (bf16[2,64,512]{2,1,0:T(8,128)(2,1)S(1)}, bf16[2,64,512]{2,1,0:T(8,128)(2,1)S(1)}, u32[]{:S(2)}, u32[]{:S(2)}) collective-permute-start(bf16[2,64,512]{2,1,0:T(8,128)(2,1)S(1)} %get-tuple-element.117), channel_id=1, source_target_pairs={{0,8},{8,0},{1,9},{9,1},{2,10},{10,2},{3,11},{11,3},{4,12},{12,4},... | collective-permute-start | bytes 393224 | tf_op jit(solution)/shard_map/ppermute | solution.py:40
  405.9 11.2 %collective-permute-start.10 = (bf16[2,64,1024]{2,1,0:T(8,128)(2,1)S(1)}, bf16[2,64,1024]{2,1,0:T(8,128)(2,1)S(1)}, u32[]{:S(2)}, u32[]{:S(2)}) collective-permute-start(bf16[2,64,1024]{2,1,0:T(8,128)(2,1)S(1)} %get-tuple-element.121), channel_id=1, source_target_pairs={{0,8},{8,0},{1,9},{9,1},{2,10},{10,2},{3,11},{11,3},{4,12},{12,4},... | collective-permute-start | bytes 786440 | tf_op jit(solution)/shard_map/ppermute | solution.py:40
  413.9 6.5 %collective-permute-start.11 = (bf16[2,64,512]{2,1,0:T(8,128)(2,1)S(1)}, bf16[2,64,512]{2,1,0:T(8,128)(2,1)S(1)}, u32[]{:S(2)}, u32[]{:S(2)}) collective-permute-start(bf16[2,64,512]{2,1,0:T(8,128)(2,1)S(1)} %get-tuple-element.115), channel_id=1, source_target_pairs={{0,8},{8,0},{1,9},{9,1},{2,10},{10,2},{3,11},{11,3},{4,12},{12,4},... | collective-permute-start | bytes 393224 | tf_op jit(solution)/shard_map/ppermute | solution.py:40
  414.6 8.7 %collective-permute-start.9 = (bf16[2,64,1024]{2,1,0:T(8,128)(2,1)S(1)}, bf16[2,64,1024]{2,1,0:T(8,128)(2,1)S(1)}, u32[]{:S(2)}, u32[]{:S(2)}) collective-permute-start(bf16[2,64,1024]{2,1,0:T(8,128)(2,1)S(1)} %get-tuple-element.119), channel_id=1, source_target_pairs={{0,8},{8,0},{1,9},{9,1},{2,10},{10,2},{3,11},{11,3},{4,12},{12,4},... | collective-permute-start | bytes 786440 | tf_op jit(solution)/shard_map/ppermute | solution.py:40
Sparse Core Ops, SparseCore 0:
  21.6 29.9 all-gather.2
  53.3 27.7 all-gather.4
  255.9 30.2 reduce-scatter.3
  288.4 41.4 reduce-scatter.7
  332.2 42.2 reduce-scatter.5
where the time goes:
time: 434 us; the launch traced here: 431 us
  waiting for transfers between devices  134 us (31%)
  blocking collectives  102 us (24%)
  Pallas kernels  76.5 us (18%)
  starting transfers between devices  57.9 us (13%)
  local copies, waits for them, and re-layouts  28.2 us (6%)
  other arithmetic  18.9 us (4%)
  between operations  14.4 us (3%)
    all_to_all x7, blocking collectives, exchange(): return lax.all_to_all(blocks, GROUP, 0, 0, tiled=True)  102 us
    all_to_all x9, waiting for transfers between devices, exchange(): return lax.all_to_all(blocks, GROUP, 0, 0, tiled=True)  76.3 us
    ppermute x13, waiting for transfers between devices, row_swap(): return lax.ppermute(value, 'row', [(0, 1), (1, 0)])  46.7 us
    all_to_all x9, starting transfers between devices, exchange(): return lax.all_to_all(blocks, GROUP, 0, 0, tiled=True)  37.4 us
    pallas_call x2, Pallas kernels, experts_back(): pl.pallas_call(experts_back_kernel, name='experts_back', grid_spec=pltpu....  16 us
    ppermute x13, starting transfers between devices, row_swap(): return lax.ppermute(value, 'row', [(0, 1), (1, 0)])  15.8 us
    pallas_call x2, Pallas kernels, experts(): pl.pallas_call(experts_kernel, name='experts', grid_spec=pltpu.PrefetchSc...  14.3 us
    pallas_call x2, Pallas kernels, experts_grads(): pl.pallas_call(experts_grads_kernel, name='experts_grads', grid=(2,), in_...  11.5 us
  transfers between devices with their start and end apart: 28, of which 20 were waited for; matrix products, arithmetic and copies ran while one was open for 8% of the time, Pallas kernels for 12%

commit v1 on v0

--- a/solution.py
+++ b/solution.py
@@ -110,15 +110,15 @@
     lse_ref[...] = total
 
 
-def attend(got, heads, out_rows, cosine, sine, layer):
+def attend(got, heads, out_rows, cosine, sine):
     return pl.pallas_call(
         attend_kernel,
         name="attend",
         grid=(1,),
         in_specs=[
             whole(got.shape),
-            at_layer(heads.shape[1:], layer),
-            at_layer(out_rows.shape[1:], layer),
+            whole(heads.shape),
+            whole(out_rows.shape),
             whole(cosine.shape),
             whole(sine.shape),
         ],
@@ -208,7 +208,7 @@
                 )
 
 
-def attend_back(row, low, got, heads, out_rows, cosine, sine, saved, router_grad, gain, layer):
+def attend_back(row, low, got, heads, out_rows, cosine, sine, saved, router_grad, gain):
     qkv, attended, total = saved
     send = (PEERS, OWN_TOKENS, MODEL_WIDTH + 128)
     return pl.pallas_call(
@@ -220,8 +220,8 @@
             in_specs=[
                 whole(low.shape),
                 whole(got.shape),
-                at_layer(heads.shape[1:], layer),
-                at_layer(out_rows.shape[1:], layer),
+                whole(heads.shape),
+                whole(out_rows.shape),
                 whole(cosine.shape),
                 whole(sine.shape),
                 whole(qkv.shape),
@@ -589,6 +589,10 @@
     )(got, hidden, gain, grad, *([] if mixed is None else [mixed]))
 
 
+def after(value):
+    return (value.reshape(-1)[0].astype(F32) > 1e30).astype(jnp.int32)
+
+
 def exchange(blocks):
     return lax.all_to_all(blocks, GROUP, 0, 0, tiled=True)
 
@@ -637,16 +641,19 @@
         [hidden_in * scale_all * gain_first, got[:, :HALF].astype(F32) * scale_all], axis=1
     ).astype(BF16)
 
-    q_low = query_key_value_weight[:, :, :HEAD_SIZE]
-    q_high = query_key_value_weight[:, :, HEAD_SIZE : 2 * HEAD_SIZE]
-    kv = query_key_value_weight[:, :, 2 * HEAD_SIZE :]
-    heads_own = jnp.concatenate([jnp.where(lower, q_low, q_high), kv], axis=2)
-    heads_sent = jnp.concatenate([jnp.where(lower, q_high, q_low), kv], axis=2)
-    heads = jnp.concatenate([heads_own, row_swap(heads_sent)], axis=1)
-    out_low, out_high = w_out[:, :HEAD_SIZE], w_out[:, HEAD_SIZE:]
-    out_rows = jnp.concatenate(
-        [jnp.where(lower, out_low, out_high), row_swap(jnp.where(lower, out_high, out_low))], axis=2
-    )
+    def attention_weights(layer, index):
+        first = index == 0
+        columns = query_key_value_weight[layer]
+        q_low, q_high = columns[:, :HEAD_SIZE], columns[:, HEAD_SIZE : 2 * HEAD_SIZE]
+        kv = columns[:, 2 * HEAD_SIZE :]
+        own = jnp.concatenate([jnp.where(first, q_low, q_high), kv], axis=1)
+        sent = jnp.concatenate([jnp.where(first, q_high, q_low), kv], axis=1)
+        low, high = w_out[layer, :HEAD_SIZE], w_out[layer, HEAD_SIZE:]
+        out_other = row_swap(jnp.where(first, high, low))
+        return (
+            jnp.concatenate([own, row_swap(sent)], axis=0),
+            jnp.concatenate([jnp.where(first, low, high), out_other], axis=1),
+        )
 
     mine = (r * 8 + c) * OWN_TOKENS
     theirs = ((1 - r) * 8 + c) * OWN_TOKENS
@@ -670,14 +677,16 @@
     gains = natural(gains_flat, small[2 * OWN_TOKENS : 2 * OWN_TOKENS + 4])
 
     k = lax.axis_index("dp")
-    others = []
-    for layer in range(layers):
-        up_sent = lax.dynamic_slice(w_gate_up, (layer, 2 - 2 * r + k // 4, 128 * (k % 4), 0), (1, 1, 128, 2 * FF))
-        down_sent = lax.dynamic_slice(w_down, (layer, 2 - 2 * r + k // 4, 128 * (k % 4), 0), (1, 1, 128, HALF))
+
+    def other_weights(layer, index):
+        start = (layer, 2 - 2 * index + k // 4, 128 * (k % 4), 0)
+        up_sent = lax.dynamic_slice(w_gate_up, start, (1, 1, 128, 2 * FF))
+        down_sent = lax.dynamic_slice(w_down, start, (1, 1, 128, HALF))
         piece = row_swap(jnp.concatenate([up_sent[0, 0], down_sent[0, 0]], axis=1))
-        others.append(lax.all_gather(piece, "dp", axis=0, tiled=True))
-    cot_low = cotangent.astype(BF16)
-    upstream = jnp.concatenate([cot_low, row_swap(cot_low)], axis=1)
+        return lax.all_gather(piece, "dp", axis=0, tiled=True)
+
+    weights = [attention_weights(0, r), None]
+    others = [other_weights(0, r + after(square)), None]
 
     router_rows = jnp.transpose(w_router, (0, 2, 1)).reshape(OWN_TOKENS, 256)
 
@@ -688,7 +697,7 @@
     records = []
     rows_in = normed_first.reshape(PEERS, OWN_TOKENS, MODEL_WIDTH)
     for layer in range(layers):
-        partial, *saved = attend(rows_in, heads, out_rows, cosine, sine, layer)
+        partial, *saved = attend(rows_in, *weights[layer], cosine, sine)
         got = exchange(partial)
         if layer == 0:
             middle, _, send = add_norm(got, hidden, gain_rows[1], router_rows)
@@ -701,6 +710,13 @@
             middle, _, send = add_norm(got, hidden, gain_rows[2 * layer + 1])
             got = exchange(send)
         normed_two = got
+        if layer == 0:
+            index = r + after(got[0, :1, :1])
+            weights[1] = attention_weights(1, index)
+            others[1] = other_weights(1, index)
+            cot_low = cotangent.astype(BF16)
+            cot_low = lax.dynamic_slice(cot_low, (index - r, 0), (TOKENS, HALF))
+            upstream = jnp.concatenate([cot_low, row_swap(cot_low)], axis=1)
         partial, pre, gates = experts(
             info, normed_two, routers[layer], expert_ids, w_gate_up, w_down, others[layer], layer
         )
@@ -718,6 +734,16 @@
         rec.update(mixed=mixed)
         records.append(rec)
 
+    def big_grads(pack):
+        big = lax.psum_scatter(pack, "dp", scatter_dimension=0, tiled=True)[0]
+        big = big.reshape(2, 192, MODEL_WIDTH)
+        up_pieces = big[:, :128].reshape(2, 2, 64, MODEL_WIDTH)
+        down_pieces = big[:, 128:]
+        up_other = row_swap(up_pieces[:, 1])
+        down_other = row_swap(down_pieces[:, :, HALF:])
+        arrived = after(up_other[0, :1, :1]) + after(down_other[0, :1, :1])
+        return up_pieces[:, 0], up_other, down_pieces[:, :, :HALF], down_other, arrived
+
     packs, smalls = [None] * layers, [None] * layers
     gain_sums = [None] * 4
     for layer in reversed(range(layers)):
@@ -728,12 +754,14 @@
         )
         got = exchange(partial)
         pack, router_grad = experts_grads(rec["normed_two"], grad_pre, act, grad_y, grad_logits)
-        packs[layer] = lax.psum_scatter(pack, "dp", scatter_dimension=0, tiled=True)
+        packs[layer] = big_grads(pack)
+        if layer == 0:
+            row = row + packs[1][-1]
         grad_middle, send = middle_back(got, rec["middle"], gain_rows[2 * layer + 1], grad_tokens)
         low = exchange(send)
         send, smalls[layer], gain_sums[2 * layer + 1] = attend_back(
-            row, low, rec["normed_one"], heads, out_rows, cosine, sine, rec["saved"],
-            router_grad, gain_rows[2 * layer], layer,
+            row, low, rec["normed_one"], *weights[layer], cosine, sine, rec["saved"],
+            router_grad, gain_rows[2 * layer],
         )
         got = exchange(send)
         if layer > 0:
@@ -764,17 +792,12 @@
         else:
             mine_small = lax.psum_scatter(smalls[layer], "dp", scatter_dimension=0, tiled=True)
             mine_small = mine_small[0].astype(F32)
-        big = packs[layer][0]
-        total = mine_small[:64] + row_swap(mine_small[64:128].astype(BF16)).astype(F32)
+        up_mine, up_other, down_mine, down_other, arrived = packs[layer]
+        sent = lax.dynamic_slice(mine_small, (64 + arrived, 0), (64, 512)).astype(BF16)
+        total = mine_small[:64] + row_swap(sent).astype(F32)
         grad_qkv = total[:, :256]
         grad_out = total[:, 256:384].reshape(4, 16, 128).transpose(1, 0, 2).reshape(16, HALF)
         grad_router = lax.dynamic_slice(total, (0, 384 + 4 * c), (64, 4))
-        big = big.reshape(2, 192, MODEL_WIDTH)
-        up_pieces = big[:, :128].reshape(2, 2, 64, MODEL_WIDTH)
-        down_pieces = big[:, 128:]
-        up_other = row_swap(up_pieces[:, 1])
-        down_other = row_swap(down_pieces[:, :, HALF:])
-        up_mine, down_mine = up_pieces[:, 0], down_pieces[:, :, :HALF]
         grad_up = jnp.where(
             lower,
             jnp.concatenate([up_mine, up_other]),

time: 434 us -> 449 us (1.035)
  blocking collectives: 102 us -> 74.5 us
  waiting for transfers between devices: 134 us -> 158 us
  starting transfers between devices: 57.9 us -> 70.2 us
    all_to_all x7 -> x5, blocking collectives: 102 us -> 74.5 us  [exchange(): return lax.all_to_all(blocks, GROUP, 0, 0, tiled=True)]
    all_gather x2, waiting for transfers between devices: 0.01 us -> 14.9 us  [other_weights(): return lax.all_gather(piece, 'dp', axis=0, tiled=True)]
    all_to_all x9 -> x11, starting transfers between devices: 37.4 us -> 50.1 us  [exchange(): return lax.all_to_all(blocks, GROUP, 0, 0, tiled=True)]
    all_to_all x9 -> x11, waiting for transfers between devices: 76.3 us -> 81.2 us  [exchange(): return lax.all_to_all(blocks, GROUP, 0, 0, tiled=True)]
    ppermute x13 -> x15, waiting for transfers between devices: 46.7 us -> 50 us  [row_swap(): return lax.ppermute(value, 'row', [(0, 1), (1, 0)])]
    unnamed x46 -> x42, local copies, waits for them, and re-layouts: 10.2 us -> 11.2 us
    ppermute x13 -> x15, starting transfers between devices: 15.8 us -> 16.4 us  [row_swap(): return lax.ppermute(value, 'row', [(0, 1), (1, 0)])]
  transfers between devices with their start and end apart: 28 -> 32, of which waited for: 20 -> 21; matrix products, arithmetic and copies ran while one was open for 8% -> 7% of each run, Pallas kernels for 12% -> 12%
where the time goes in v1:
time: 449 us; the launch traced here: 446 us
  waiting for transfers between devices  158 us (35%)
  Pallas kernels  75.7 us (17%)
  blocking collectives  74.5 us (17%)
  starting transfers between devices  70.2 us (16%)
  local copies, waits for them, and re-layouts  32 us (7%)
  between operations  18.5 us (4%)
  other arithmetic  17.2 us (4%)
    all_to_all x11, waiting for transfers between devices, exchange(): return lax.all_to_all(blocks, GROUP, 0, 0, tiled=True)  81.2 us
    all_to_all x5, blocking collectives, exchange(): return lax.all_to_all(blocks, GROUP, 0, 0, tiled=True)  74.5 us
    all_to_all x11, starting transfers between devices, exchange(): return lax.all_to_all(blocks, GROUP, 0, 0, tiled=True)  50.1 us
    ppermute x15, waiting for transfers between devices, row_swap(): return lax.ppermute(value, 'row', [(0, 1), (1, 0)])  50 us
    ppermute x15, starting transfers between devices, row_swap(): return lax.ppermute(value, 'row', [(0, 1), (1, 0)])  16.4 us
    pallas_call x2, Pallas kernels, experts_back(): pl.pallas_call(experts_back_kernel, name='experts_back', grid_spec=pltpu....  15.9 us
    all_gather x2, waiting for transfers between devices, other_weights(): return lax.all_gather(piece, 'dp', axis=0, tiled=True)  14.9 us
    pallas_call x2, Pallas kernels, experts(): pl.pallas_call(experts_kernel, name='experts', grid_spec=pltpu.PrefetchSc...  14.3 us
  transfers between devices with their start and end apart: 32, of which 21 were waited for; matrix products, arithmetic and copies ran while one was open for 7% of the time, Pallas kernels for 12%

profile of v1, /device:TPU:0, one launch (start us, length us, event | category | flops | bytes accessed | tf_op | source)
XLA Modules:
  0.0 446.2 jit_solution(11620380822592574554)
XLA Ops:
  9.7 2.0 collective-permute-start.3
  14.6 2.1 collective-permute-start
  19.1 10.2 %collective-permute-done.2 = bf16[64,512]{1,0:T(8,128)(2,1)S(1)} collective-permute-done((bf16[64,512]{1,0:T(8,128)(2,1)S(1)}, bf16[64,512]{1,0:T(8,128)(2,1)S(1)}, u32[]{:S(2)}, u32[]{:S(2)}) %collective-permute-start.2) | collective-permute-done | bytes 65568 | tf_op jit(solution)/shard_map/ppermute | solution.py:40
  32.3 3.3 attend.2
  35.6 7.4 %all-to-all-start = ((bf16[16,16,1024]{2,1,0:T(8,128)(2,1)}), bf16[16,16,1024]{2,1,0:T(8,128)(2,1)S(1)}, u32[]{:S(2)}, u32[]{:S(2)}) async-start(bf16[16,16,1024]{2,1,0:T(8,128)(2,1)} %get-tuple-element.59), calls=%async_computation | async-start | bytes 1048576 | tf_op jit(solution)/shard_map/all_to_all | solution.py:597
  44.3 9.0 %all-to-all-done.got_ref = bf16[16,16,1024]{2,1,0:T(8,128)(2,1)S(1)} async-done(((bf16[16,16,1024]{2,1,0:T(8,128)(2,1)}), bf16[16,16,1024]{2,1,0:T(8,128)(2,1)S(1)}, u32[]{:S(2)}, u32[]{:S(2)}) %all-to-all-start) | async-done | bytes 524320 | tf_op jit(solution)/shard_map/all_to_all | solution.py:597
  54.1 2.1 add_norm.3
  56.2 3.6 all-to-all-start.1
  61.1 9.6 %all-to-all-done.1.x_ref = bf16[16,16,1280]{2,1,0:T(8,128)(2,1)S(1)} async-done(((bf16[16,16,1280]{2,1,0:T(8,128)(2,1)}), bf16[16,16,1280]{2,1,0:T(8,128)(2,1)S(1)}, u32[]{:S(2)}, u32[]{:S(2)}) %all-to-all-start.1) | async-done | bytes 655392 | tf_op jit(solution)/shard_map/all_to_all | solution.py:597
  74.4 8.7 %collective-permute-done.4 = bf16[128,1536]{1,0:T(8,128)(2,1)S(1)} collective-permute-done((bf16[128,1536]{1,0:T(8,128)(2,1)S(1)}, bf16[128,1536]{1,0:T(8,128)(2,1)S(1)}, u32[]{:S(2)}, u32[]{:S(2)}) %collective-permute-start.4) | collective-permute-done | bytes 393248 | tf_op jit(solution)/shard_map/ppermute | solution.py:40
  84.0 7.8 %collective-permute-done.7 = bf16[128,1536]{1,0:T(8,128)(2,1)S(1)} collective-permute-done((bf16[128,1536]{1,0:T(8,128)(2,1)S(1)}, bf16[128,1536]{1,0:T(8,128)(2,1)S(1)}, u32[]{:S(2)}, u32[]{:S(2)}) %collective-permute-start.7) | collective-permute-done | bytes 393248 | tf_op jit(solution)/shard_map/ppermute | solution.py:40
  94.9 14.9 %all-gather.3.cloned.1.call-done.other_ref = bf16[1024,1536]{1,0:T(8,128)(2,1)} async-done(((bf16[128,1536]{1,0:T(8,128)(2,1)}), bf16[1024,1536]{1,0:T(8,128)(2,1)}) %all-gather.3.cloned.1.call-update) | async-done | bytes 3145744 | tf_op jit(solution)/shard_map/all_gather | solution.py:686
  109.9 7.1 %experts.2 = (bf16[16,16,1024]{2,1,0:T(8,128)(2,1)}, f32[2,256,1024]{2,1,0:T(8,128)}, f32[256,32]{1,0:T(8,128)}) custom-call(s32[2]{0:T(128)} %pad_add_fusion.info_ref, bf16[16,16,1280]{2,1,0:T(8,128)(2,1)} %copy-done.1, bf16[32,1024]{1,0:T(8,128)(2,1)} %bitcast.112, s32[2,256,8]{2,1,0:T(8,128)} %copy.34.ids_ref, bf16[2,4,512,1024]{3,2,1,0:T(8,128)(2,1)} %up_ref.7, ...), custom_call_target="tpu_custom_call" | custom-call | flops 1600000000 | bytes 9000000 | tf_op jit(solution)/shard_map/experts/pallas_call | solution.py:298
  117.0 6.9 %all-to-all-start.2 = ((bf16[16,16,1024]{2,1,0:T(8,128)(2,1)}), bf16[16,16,1024]{2,1,0:T(8,128)(2,1)S(1)}, u32[]{:S(2)}, u32[]{:S(2)}) async-start(bf16[16,16,1024]{2,1,0:T(8,128)(2,1)} %get-tuple-element.61), calls=%async_computation.2 | async-start | bytes 1048576 | tf_op jit(solution)/shard_map/all_to_all | solution.py:597
  124.2 2.0 collective-permute-start.5
  126.2 9.6 %all-to-all-done.2.got_ref = bf16[16,16,1024]{2,1,0:T(8,128)(2,1)S(1)} async-done(((bf16[16,16,1024]{2,1,0:T(8,128)(2,1)}), bf16[16,16,1024]{2,1,0:T(8,128)(2,1)S(1)}, u32[]{:S(2)}, u32[]{:S(2)}) %all-to-all-start.2) | async-done | bytes 524320 | tf_op jit(solution)/shard_map/all_to_all | solution.py:597
  136.6 2.1 add_norm.4
  138.7 3.7 all-to-all-start.3
  142.4 2.0 collective-permute-start.6
  144.4 5.5 %collective-permute-done.6 = bf16[64,512]{1,0:T(8,128)(2,1)S(1)} collective-permute-done((bf16[64,512]{1,0:T(8,128)(2,1)S(1)}, bf16[64,512]{1,0:T(8,128)(2,1)S(1)}, u32[]{:S(2)}, u32[]{:S(2)}) %collective-permute-start.6) | collective-permute-done | bytes 65568 | tf_op jit(solution)/shard_map/ppermute | solution.py:40
  151.5 1.6 all-to-all-done.3.x_ref
  154.0 3.3 attend.3
  157.3 17.2 %all_to_all.85.got_ref = bf16[16,16,1024]{2,1,0:T(8,128)(2,1)} all-to-all(bf16[16,16,1024]{2,1,0:T(8,128)(2,1)} %get-tuple-element.64), channel_id=1, replica_groups=mesh['dp'=8,'row'=2,'col'=8] {'row','col'}, dimensions={0} | all-to-all | bytes 1048576 | tf_op jit(solution)/shard_map/all_to_all | solution.py:597
  174.5 2.1 add_norm.5
  176.6 3.8 all-to-all-start.5
  181.1 9.6 %all-to-all-done.5.x_ref = bf16[16,16,1024]{2,1,0:T(8,128)(2,1)S(1)} async-done(((bf16[16,16,1024]{2,1,0:T(8,128)(2,1)}), bf16[16,16,1024]{2,1,0:T(8,128)(2,1)S(1)}, u32[]{:S(2)}, u32[]{:S(2)}) %all-to-all-start.5) | async-done | bytes 524320 | tf_op jit(solution)/shard_map/all_to_all | solution.py:597
  191.5 7.2 %experts.3 = (bf16[16,16,1024]{2,1,0:T(8,128)(2,1)}, f32[2,256,1024]{2,1,0:T(8,128)}, f32[256,32]{1,0:T(8,128)}) custom-call(s32[2]{0:T(128)} %pad_add_fusion.info_ref, bf16[16,16,1024]{2,1,0:T(8,128)(2,1)} %copy-done.5, bf16[32,1024]{1,0:T(8,128)(2,1)} %bitcast.114, s32[2,256,8]{2,1,0:T(8,128)} %copy.34.ids_ref, bf16[2,4,512,1024]{3,2,1,0:T(8,128)(2,1)} %up_ref.7, ...), custom_call_target="tpu_custom_call" | custom-call | flops 1600000000 | bytes 9000000 | tf_op jit(solution)/shard_map/experts/pallas_call | solution.py:298
  198.7 3.6 all-to-all-start.6
  202.3 1.9 collective-permute-start.8
  204.9 7.5 %all-to-all-done.6.got_ref = bf16[16,16,1024]{2,1,0:T(8,128)(2,1)S(1)} async-done(((bf16[16,16,1024]{2,1,0:T(8,128)(2,1)}), bf16[16,16,1024]{2,1,0:T(8,128)(2,1)S(1)}, u32[]{:S(2)}, u32[]{:S(2)}) %all-to-all-start.6) | async-done | bytes 524320 | tf_op jit(solution)/shard_map/all_to_all | solution.py:597
  213.2 2.0 add_last.1
  215.2 3.9 all-to-all-start.7
  220.0 8.1 %all-to-all-done.7 = bf16[16,16,640]{2,1,0:T(8,128)(2,1)S(1)} async-done(((bf16[16,16,640]{2,1,0:T(8,128)(2,1)}), bf16[16,16,640]{2,1,0:T(8,128)(2,1)S(1)}, u32[]{:S(2)}, u32[]{:S(2)}) %all-to-all-start.7) | async-done | bytes 327712 | tf_op jit(solution)/shard_map/all_to_all | solution.py:597
  228.8 8.0 %experts_back.2 = (bf16[16,16,1024]{2,1,0:T(8,128)(2,1)}, bf16[2,256,1024]{2,1,0:T(8,128)(2,1)}, bf16[2,256,512]{2,1,0:T(8,128)(2,1)}, bf16[2,256,1024]{2,1,0:T(8,128)(2,1)}, f32[256,32]{1,0:T(8,128)}) custom-call(s32[2]{0:T(128)} %pad_add_fusion.info_ref, bf16[256,1024]{1,0:T(8,128)(2,1)} %pad_maximum_fusion.3.g_ref, bf16[256,128]{1,0:T(8,128)(2,1)} %slice.282.mean_ref, ...), custom_call_target="tpu_custom_call" | custom-call | flops 1700000000 | bytes 11000000 | tf_op jit(solution)/shard_map/experts_back/pallas_call | solution.py:375
  236.8 5.8 %experts_grads.2 = (bf16[8,384,1024]{2,1,0:T(8,128)(2,1)}, f32[1024,32]{1,0:T(8,128)}) custom-call(bf16[16,16,1024]{2,1,0:T(8,128)(2,1)} %copy-done.5, bf16[2,256,1024]{2,1,0:T(8,128)(2,1)} %get-tuple-element.72.grad_pre_ref, bf16[2,256,512]{2,1,0:T(8,128)(2,1)} %get-tuple-element.73.act_ref, bf16[2,256,1024]{2,1,0:T(8,128)(2,1)} %get-tuple-element.74.grad_y_ref, ...), custom_call_target="tpu_custom_call" | custom-call | flops 1600000000 | bytes 9000000 | tf_op jit(solution)/shard_map/experts_grads/pallas_call | solution.py:427
  243.6 13.3 %all_to_all.86.got_ref = bf16[16,16,1024]{2,1,0:T(8,128)(2,1)} all-to-all(bf16[16,16,1024]{2,1,0:T(8,128)(2,1)S(1)} %copy-done.11), channel_id=1, replica_groups=mesh['dp'=8,'row'=2,'col'=8] {'row','col'}, dimensions={0} | all-to-all | bytes 1048576 | tf_op jit(solution)/shard_map/all_to_all | solution.py:597
  256.9 2.2 middle_back.2
  259.0 14.9 %all_to_all.87.low_ref = bf16[16,16,1152]{2,1,0:T(8,128)(2,1)} all-to-all(bf16[16,16,1152]{2,1,0:T(8,128)(2,1)} %get-tuple-element.78), channel_id=1, replica_groups=mesh['dp'=8,'row'=2,'col'=8] {'row','col'}, dimensions={0} | all-to-all | bytes 1179648 | tf_op jit(solution)/shard_map/all_to_all | solution.py:597
  273.9 5.3 %attend_back.2 = (bf16[16,16,1152]{2,1,0:T(8,128)(2,1)}, bf16[8,144,512]{2,1,0:T(8,128)(2,1)}, f32[16,128]{1,0:T(8,128)}) custom-call(s32[1]{0:T(128)} %bitcast.row_ref, bf16[16,16,1152]{2,1,0:T(8,128)(2,1)} %all_to_all.87.low_ref, bf16[16,16,1024]{2,1,0:T(8,128)(2,1)} %copy-done, bf16[1024,192]{1,0:T(8,128)(2,1)} %pad_maximum_fusion.2.heads_ref, ...), custom_call_target="tpu_custom_call" | custom-call | flops 500000000 | bytes 4000000 | tf_op jit(solution)/shard_map/attend_back/pallas_call | solution.py:214
  279.3 14.9 %all_to_all.88.got_ref = bf16[16,16,1152]{2,1,0:T(8,128)(2,1)} all-to-all(bf16[16,16,1152]{2,1,0:T(8,128)(2,1)} %get-tuple-element.83), channel_id=1, replica_groups=mesh['dp'=8,'row'=2,'col'=8] {'row','col'}, dimensions={0} | all-to-all | bytes 1179648 | tf_op jit(solution)/shard_map/all_to_all | solution.py:597
  294.2 2.2 first_back.2
  296.4 14.2 %all_to_all.89 = bf16[16,16,1152]{2,1,0:T(8,128)(2,1)S(1)} all-to-all(bf16[16,16,1152]{2,1,0:T(8,128)(2,1)} %get-tuple-element.86), channel_id=1, replica_groups=mesh['dp'=8,'row'=2,'col'=8] {'row','col'}, dimensions={0} | all-to-all | bytes 1179648 | tf_op jit(solution)/shard_map/all_to_all | solution.py:597
  312.1 8.0 %experts_back.3 = (bf16[16,16,1024]{2,1,0:T(8,128)(2,1)}, bf16[2,256,1024]{2,1,0:T(8,128)(2,1)}, bf16[2,256,512]{2,1,0:T(8,128)(2,1)}, bf16[2,256,1024]{2,1,0:T(8,128)(2,1)}, f32[256,32]{1,0:T(8,128)}) custom-call(s32[2]{0:T(128)} %pad_add_fusion.info_ref, bf16[256,1024]{1,0:T(8,128)(2,1)} %bitcast.101, bf16[256,128]{1,0:T(8,128)(2,1)} %bitcast.118, ...), custom_call_target="tpu_custom_call" | custom-call | flops 1700000000 | bytes 11000000 | tf_op jit(solution)/shard_map/experts_back/pallas_call | solution.py:375
  320.1 5.8 %experts_grads.3 = (bf16[8,384,1024]{2,1,0:T(8,128)(2,1)}, f32[1024,32]{1,0:T(8,128)}) custom-call(bf16[16,16,1280]{2,1,0:T(8,128)(2,1)} %copy-done.1, bf16[2,256,1024]{2,1,0:T(8,128)(2,1)} %get-tuple-element.95.grad_pre_ref, bf16[2,256,512]{2,1,0:T(8,128)(2,1)} %get-tuple-element.96.act_ref, bf16[2,256,1024]{2,1,0:T(8,128)(2,1)} %get-tuple-element.97.grad_y_ref, ...), custom_call_target="tpu_custom_call" | custom-call | flops 1600000000 | bytes 9000000 | tf_op jit(solution)/shard_map/experts_grads/pallas_call | solution.py:427
  325.9 3.8 all-to-all-start.12
  329.7 9.7 %all-to-all-done.12.got_ref = bf16[16,16,1024]{2,1,0:T(8,128)(2,1)S(1)} async-done(((bf16[16,16,1024]{2,1,0:T(8,128)(2,1)}), bf16[16,16,1024]{2,1,0:T(8,128)(2,1)S(1)}, u32[]{:S(2)}, u32[]{:S(2)}) %all-to-all-start.12) | async-done | bytes 524320 | tf_op jit(solution)/shard_map/all_to_all | solution.py:597
  340.2 2.2 middle_back.3
  342.4 3.6 all-to-all-start.13
  347.1 2.0 collective-permute-start.9
  351.2 6.2 %collective-permute-done.10 = bf16[2,64,512]{2,1,0:T(8,128)(2,1)S(1)} collective-permute-done((bf16[2,64,512]{2,1,0:T(8,128)(2,1)S(1)}, bf16[2,64,512]{2,1,0:T(8,128)(2,1)S(1)}, u32[]{:S(2)}, u32[]{:S(2)}) %collective-permute-start.10) | collective-permute-done | bytes 131104 | tf_op jit(solution)/shard_map/ppermute | solution.py:40
  360.5 5.3 %attend_back.3 = (bf16[16,16,1152]{2,1,0:T(8,128)(2,1)}, bf16[8,144,512]{2,1,0:T(8,128)(2,1)}, f32[16,128]{1,0:T(8,128)}) custom-call(s32[1]{0:T(128)S(6)} %add.167.row_ref, bf16[16,16,1152]{2,1,0:T(8,128)(2,1)} %copy-done.4, bf16[16,16,1024]{2,1,0:T(8,128)(2,1)} %pad_maximum_fusion.x_ref, bf16[1024,192]{1,0:T(8,128)(2,1)} %pad_maximum_fusion.1.heads_ref, ...), custom_call_target="tpu_custom_call" | custom-call | flops 500000000 | bytes 4000000 | tf_op jit(solution)/shard_map/attend_back/pallas_call | solution.py:214
  365.9 6.0 %all-to-all-start.14 = ((bf16[16,16,1152]{2,1,0:T(8,128)(2,1)}), bf16[16,16,1152]{2,1,0:T(8,128)(2,1)S(1)}, u32[]{:S(2)}, u32[]{:S(2)}) async-start(bf16[16,16,1152]{2,1,0:T(8,128)(2,1)} %get-tuple-element.100), calls=%async_computation.15 | async-start | bytes 1179648 | tf_op jit(solution)/shard_map/all_to_all | solution.py:597
  373.6 9.0 %all-to-all-done.14.got_ref = bf16[16,16,1152]{2,1,0:T(8,128)(2,1)S(1)} async-done(((bf16[16,16,1152]{2,1,0:T(8,128)(2,1)}), bf16[16,16,1152]{2,1,0:T(8,128)(2,1)S(1)}, u32[]{:S(2)}, u32[]{:S(2)}) %all-to-all-start.14) | async-done | bytes 589856 | tf_op jit(solution)/shard_map/all_to_all | solution.py:597
  383.4 2.0 first_back.3
  385.4 3.7 all-to-all-start.15
  390.6 7.4 %all-to-all-done.15 = bf16[16,16,512]{2,1,0:T(8,128)(2,1)S(1)} async-done(((bf16[16,16,512]{2,1,0:T(8,128)(2,1)}), bf16[16,16,512]{2,1,0:T(8,128)(2,1)S(1)}, u32[]{:S(2)}, u32[]{:S(2)}) %all-to-all-start.15) | async-done | bytes 262176 | tf_op jit(solution)/shard_map/all_to_all | solution.py:597
  398.0 3.6 all-to-all-start.16
  402.3 3.8 collective-permute-done.14
  407.1 11.7 %all-to-all-done.16 = bf16[8,144,512]{2,1,0:T(8,128)(2,1)S(1)} async-done(((bf16[8,144,512]{2,1,0:T(8,128)(2,1)}), bf16[8,144,512]{2,1,0:T(8,128)(2,1)S(1)}, u32[]{:S(2)}, u32[]{:S(2)}) %all-to-all-start.16) | async-done | bytes 1179680 | tf_op jit(solution)/shard_map/all_to_all | solution.py:786
  421.9 1.5 collective-permute-start.11
  424.0 3.7 collective-permute-done.12
  429.9 2.0 collective-permute-done.11
  433.9 1.5 maximum_convert_fusion
  435.3 2.2 collective-permute-done.13
  (181 shorter events, 50.9 us)
Async XLA Ops:
  7.2 6.0 %copy-start.2 = (f32[256,512]{1,0:T(8,128)S(1)}, f32[256,512]{1,0:T(8,128)}, u32[]{:S(2)}) copy-start(f32[256,512]{1,0:T(8,128)} %param.9) | copy-start | bytes 1572868
  9.7 33.4 %collective-permute-start.3 = (f32[40,512]{1,0:T(8,128)S(1)}, f32[40,512]{1,0:T(8,128)S(1)}, u32[]{:S(2)}, u32[]{:S(2)}) collective-permute-start(f32[40,512]{1,0:T(8,128)S(1)} %maximum_maximum_fusion.1), channel_id=1, source_target_pairs={{0,8},{8,0},{1,9},{9,1},{2,10},{10,2},{3,11},{11,3},{4,12},{12,4},... | collective-permute-start | bytes 245768 | tf_op jit(solution)/shard_map/ppermute | solution.py:40
  12.8 3.9 copy-start.14
  13.1 5.5 %copy-start.18 = (bf16[2,512,4]{1,2,0:T(4,128)(2,1)S(1)}, bf16[2,512,4]{1,2,0:T(4,128)(2,1)}, u32[]{:S(2)}) copy-start(bf16[2,512,4]{1,2,0:T(4,128)(2,1)} %param.14) | copy-start | bytes 24580
  13.1 16.9 %collective-permute-start.1 = (bf16[512,192]{1,0:T(8,128)(2,1)S(1)}, bf16[512,192]{1,0:T(8,128)(2,1)S(1)}, u32[]{:S(2)}, u32[]{:S(2)}) collective-permute-start(bf16[512,192]{1,0:T(8,128)(2,1)S(1)} %pad_maximum_fusion.6), channel_id=1, source_target_pairs={{0,8},{8,0},{1,9},{9,1},{2,10},{10,2},{3,11},{11,3},{4,12},{12,4},... | collective-permute-start | bytes 589832 | tf_op jit(solution)/shard_map/ppermute | solution.py:40
  14.6 16.4 %collective-permute-start = (bf16[256,640]{0,1:T(8,128)(2,1)S(1)}, bf16[256,640]{0,1:T(8,128)(2,1)S(1)}, u32[]{:S(2)}, u32[]{:S(2)}) collective-permute-start(bf16[256,640]{0,1:T(8,128)(2,1)S(1)} %maximum_maximum_fusion), channel_id=1, source_target_pairs={{0,8},{8,0},{1,9},{9,1},{2,10},{10,2},{3,11},{11,3},{4,12},{12,4},... | collective-permute-start | bytes 983048 | tf_op jit(solution)/shard_map/ppermute | solution.py:40
  16.7 12.7 %collective-permute-start.2 = (bf16[64,512]{1,0:T(8,128)(2,1)S(1)}, bf16[64,512]{1,0:T(8,128)(2,1)S(1)}, u32[]{:S(2)}, u32[]{:S(2)}) collective-permute-start(bf16[64,512]{1,0:T(8,128)(2,1)S(1)} %get-tuple-element.135), channel_id=1, source_target_pairs={{0,8},{8,0},{1,9},{9,1},{2,10},{10,2},{3,11},{11,3},{4,12},{12,4},... | collective-permute-start | bytes 196616 | tf_op jit(solution)/shard_map/ppermute | solution.py:40
  35.6 17.7 %all-to-all-start = ((bf16[16,16,1024]{2,1,0:T(8,128)(2,1)}), bf16[16,16,1024]{2,1,0:T(8,128)(2,1)S(1)}, u32[]{:S(2)}, u32[]{:S(2)}) async-start(bf16[16,16,1024]{2,1,0:T(8,128)(2,1)} %get-tuple-element.59), calls=%async_computation | async-start | bytes 1048576 | tf_op jit(solution)/shard_map/all_to_all | solution.py:597
  53.3 0.8 copy-start.8
  56.2 14.5 %all-to-all-start.1 = ((bf16[16,16,1280]{2,1,0:T(8,128)(2,1)}), bf16[16,16,1280]{2,1,0:T(8,128)(2,1)S(1)}, u32[]{:S(2)}, u32[]{:S(2)}) async-start(bf16[16,16,1280]{2,1,0:T(8,128)(2,1)} %get-tuple-element.60), calls=%async_computation.1 | async-start | bytes 1310720 | tf_op jit(solution)/shard_map/all_to_all | solution.py:597
  59.8 32.8 %copy-start.15 = (s32[2,256,8]{1,2,0:T(8,128)S(1)}, s32[2,256,8]{1,2,0:T(8,128)}, u32[]{:S(2)}) copy-start(s32[2,256,8]{1,2,0:T(8,128)} %param.17) | copy-start | bytes 49156
  59.8 50.1 %all-gather.3.cloned.1.call-start = ((), (), s32[]{:S(2)}) async-start(), calls=%async_computation.20 | async-start | bytes 3538944 | tf_op jit(solution)/shard_map/all_gather | solution.py:686
  70.7 23.3 %copy-start.1 = (bf16[16,16,1280]{2,1,0:T(8,128)(2,1)}, bf16[16,16,1280]{2,1,0:T(8,128)(2,1)S(1)}, u32[]{:S(2)}) copy-start(bf16[16,16,1280]{2,1,0:T(8,128)(2,1)S(1)} %all-to-all-done.1.x_ref) | copy-start | bytes 1966084
  74.0 9.1 %collective-permute-start.4 = (bf16[128,1536]{1,0:T(8,128)(2,1)S(1)}, bf16[128,1536]{1,0:T(8,128)(2,1)S(1)}, u32[]{:S(2)}, u32[]{:S(2)}) collective-permute-start(bf16[128,1536]{1,0:T(8,128)(2,1)S(1)} %pad_maximum_fusion.4), channel_id=1, source_target_pairs={{0,8},{8,0},{1,9},{9,1},{2,10},{10,2},{3,11},{11,3},{4,12},{12,4},... | collective-permute-start | bytes 1179656 | tf_op jit(solution)/shard_map/ppermute | solution.py:40
  83.1 0.7 copy-start.13
  83.9 97.2 %all-gather.5.cloned.1.call-start = ((), (), s32[]{:S(2)}) async-start(), calls=%async_computation.21 | async-start | bytes 3538944 | tf_op jit(solution)/shard_map/all_gather | solution.py:686
  84.0 7.9 %collective-permute-start.7 = (bf16[128,1536]{1,0:T(8,128)(2,1)S(1)}, bf16[128,1536]{1,0:T(8,128)(2,1)S(1)}, u32[]{:S(2)}, u32[]{:S(2)}) collective-permute-start(bf16[128,1536]{1,0:T(8,128)(2,1)S(1)} %pad_maximum_fusion.5), channel_id=1, source_target_pairs={{0,8},{8,0},{1,9},{9,1},{2,10},{10,2},{3,11},{11,3},{4,12},{12,4},... | collective-permute-start | bytes 1179656 | tf_op jit(solution)/shard_map/ppermute | solution.py:40
  91.8 0.8 copy-start.12
  117.0 18.9 %all-to-all-start.2 = ((bf16[16,16,1024]{2,1,0:T(8,128)(2,1)}), bf16[16,16,1024]{2,1,0:T(8,128)(2,1)S(1)}, u32[]{:S(2)}, u32[]{:S(2)}) async-start(bf16[16,16,1024]{2,1,0:T(8,128)(2,1)} %get-tuple-element.61), calls=%async_computation.2 | async-start | bytes 1048576 | tf_op jit(solution)/shard_map/all_to_all | solution.py:597
  124.2 26.4 %collective-permute-start.5 = (bf16[512,192]{1,0:T(8,128)(2,1)S(1)}, bf16[512,192]{1,0:T(8,128)(2,1)S(1)}, u32[]{:S(2)}, u32[]{:S(2)}) collective-permute-start(bf16[512,192]{1,0:T(8,128)(2,1)S(1)} %pad_maximum_fusion.7), channel_id=1, source_target_pairs={{0,8},{8,0},{1,9},{9,1},{2,10},{10,2},{3,11},{11,3},{4,12},{12,4},... | collective-permute-start | bytes 589832 | tf_op jit(solution)/shard_map/ppermute | solution.py:40
  135.8 0.8 copy-start.9
  138.7 14.5 %all-to-all-start.3 = ((bf16[16,16,1024]{2,1,0:T(8,128)(2,1)}), bf16[16,16,1024]{2,1,0:T(8,128)(2,1)S(1)}, u32[]{:S(2)}, u32[]{:S(2)}) async-start(bf16[16,16,1024]{2,1,0:T(8,128)(2,1)} %get-tuple-element.63), calls=%async_computation.3 | async-start | bytes 1048576 | tf_op jit(solution)/shard_map/all_to_all | solution.py:597
  142.4 7.5 %collective-permute-start.6 = (bf16[64,512]{1,0:T(8,128)(2,1)S(1)}, bf16[64,512]{1,0:T(8,128)(2,1)S(1)}, u32[]{:S(2)}, u32[]{:S(2)}) collective-permute-start(bf16[64,512]{1,0:T(8,128)(2,1)S(1)} %get-tuple-element.131), channel_id=1, source_target_pairs={{0,8},{8,0},{1,9},{9,1},{2,10},{10,2},{3,11},{11,3},{4,12},{12,4},... | collective-permute-start | bytes 196616 | tf_op jit(solution)/shard_map/ppermute | solution.py:40
  153.2 0.8 copy-start
  176.6 14.1 %all-to-all-start.5 = ((bf16[16,16,1024]{2,1,0:T(8,128)(2,1)}), bf16[16,16,1024]{2,1,0:T(8,128)(2,1)S(1)}, u32[]{:S(2)}, u32[]{:S(2)}) async-start(bf16[16,16,1024]{2,1,0:T(8,128)(2,1)} %get-tuple-element.66), calls=%async_computation.5 | async-start | bytes 1048576 | tf_op jit(solution)/shard_map/all_to_all | solution.py:597
  190.7 0.8 copy-start.5
  191.5 10.8 %copy-start.10 = (f32[256,512]{1,0:T(8,128)S(1)}, f32[256,512]{1,0:T(8,128)}, u32[]{:S(2)}) copy-start(f32[256,512]{1,0:T(8,128)} %param.10) | copy-start | bytes 1572868
  198.7 13.7 %all-to-all-start.6 = ((bf16[16,16,1024]{2,1,0:T(8,128)(2,1)}), bf16[16,16,1024]{2,1,0:T(8,128)(2,1)S(1)}, u32[]{:S(2)}, u32[]{:S(2)}) async-start(bf16[16,16,1024]{2,1,0:T(8,128)(2,1)} %get-tuple-element.67), calls=%async_computation.6 | async-start | bytes 1048576 | tf_op jit(solution)/shard_map/all_to_all | solution.py:597
  202.3 16.8 %collective-permute-start.8 = (bf16[256,512]{1,0:T(8,128)(2,1)S(1)}, bf16[256,512]{1,0:T(8,128)(2,1)S(1)}, u32[]{:S(2)}, u32[]{:S(2)}) collective-permute-start(bf16[256,512]{1,0:T(8,128)(2,1)S(1)} %convert_element_type.168), channel_id=1, source_target_pairs={{0,8},{8,0},{1,9},{9,1},{2,10},{10,2},{3,11},{11,3},{4,12},{12,4},... | collective-permute-start | bytes 786440 | tf_op jit(solution)/shard_map/ppermute | solution.py:40
  212.4 0.8 copy-start.7
  215.2 13.0 %all-to-all-start.7 = ((bf16[16,16,640]{2,1,0:T(8,128)(2,1)}), bf16[16,16,640]{2,1,0:T(8,128)(2,1)S(1)}, u32[]{:S(2)}, u32[]{:S(2)}) async-start(bf16[16,16,640]{2,1,0:T(8,128)(2,1)} %get-tuple-element.69), calls=%async_computation.7 | async-start | bytes 655360 | tf_op jit(solution)/shard_map/all_to_all | solution.py:597
  219.1 126.9 %reduce-scatter.4.cloned.1.call-start = ((), (), s32[]{:S(2)}) async-start(), calls=%async_computation.22 | async-start | bytes 7077888 | tf_op jit(solution)/shard_map/reduce_scatter | solution.py:738
  242.5 1.0 copy-start.11
  242.6 129.4 %reduce-scatter.8.cloned.1.call-start = ((), (), s32[]{:S(2)}) async-start(), calls=%async_computation.24 | async-start | bytes 1327104 | tf_op jit(solution)/shard_map/reduce_scatter | solution.py:793
  279.3 139.8 %reduce-scatter.6.cloned.1.call-start = ((), (), s32[]{:S(2)}) async-start(), calls=%async_computation.23 | async-start | bytes 7077888 | tf_op jit(solution)/shard_map/reduce_scatter | solution.py:738
  325.9 13.5 %all-to-all-start.12 = ((bf16[16,16,1024]{2,1,0:T(8,128)(2,1)}), bf16[16,16,1024]{2,1,0:T(8,128)(2,1)S(1)}, u32[]{:S(2)}, u32[]{:S(2)}) async-start(bf16[16,16,1024]{2,1,0:T(8,128)(2,1)} %get-tuple-element.89), calls=%async_computation.13 | async-start | bytes 1048576 | tf_op jit(solution)/shard_map/all_to_all | solution.py:597
  339.4 0.8 copy-start.6
  342.4 17.3 %all-to-all-start.13 = ((bf16[16,16,1152]{2,1,0:T(8,128)(2,1)}), bf16[16,16,1152]{2,1,0:T(8,128)(2,1)S(1)}, u32[]{:S(2)}, u32[]{:S(2)}) async-start(bf16[16,16,1152]{2,1,0:T(8,128)(2,1)} %get-tuple-element.91), calls=%async_computation.14 | async-start | bytes 1179648 | tf_op jit(solution)/shard_map/all_to_all | solution.py:597
  347.1 11.4 %collective-permute-start.9 = (bf16[2,64,1024]{2,1,0:T(8,128)(2,1)S(1)}, bf16[2,64,1024]{2,1,0:T(8,128)(2,1)S(1)}, u32[]{:S(2)}, u32[]{:S(2)}) collective-permute-start(bf16[2,64,1024]{2,1,0:T(8,128)(2,1)S(1)} %get-tuple-element.123), channel_id=1, source_target_pairs={{0,8},{8,0},{1,9},{9,1},{2,10},{10,2},{3,11},{11,3},{4,12},{12,4},... | collective-permute-start | bytes 786440 | tf_op jit(solution)/shard_map/ppermute | solution.py:40
  350.1 7.2 %collective-permute-start.10 = (bf16[2,64,512]{2,1,0:T(8,128)(2,1)S(1)}, bf16[2,64,512]{2,1,0:T(8,128)(2,1)S(1)}, u32[]{:S(2)}, u32[]{:S(2)}) collective-permute-start(bf16[2,64,512]{2,1,0:T(8,128)(2,1)S(1)} %get-tuple-element.119), channel_id=1, source_target_pairs={{0,8},{8,0},{1,9},{9,1},{2,10},{10,2},{3,11},{11,3},{4,12},{12,4},... | collective-permute-start | bytes 393224 | tf_op jit(solution)/shard_map/ppermute | solution.py:40
  351.2 20.8 %copy-start.16 = (f32[16,128]{1,0:T(8,128)S(1)}, f32[16,128]{1,0:T(8,128)}, u32[]{:S(2)}) copy-start(f32[16,128]{1,0:T(8,128)} %get-tuple-element.107) | copy-start | bytes 24580
  351.2 20.8 %copy-start.17 = (f32[16,128]{1,0:T(8,128)S(1)}, f32[16,128]{1,0:T(8,128)}, u32[]{:S(2)}) copy-start(f32[16,128]{1,0:T(8,128)} %get-tuple-element.106) | copy-start | bytes 24580
  359.7 0.8 copy-start.4
  365.9 16.7 %all-to-all-start.14 = ((bf16[16,16,1152]{2,1,0:T(8,128)(2,1)}), bf16[16,16,1152]{2,1,0:T(8,128)(2,1)S(1)}, u32[]{:S(2)}, u32[]{:S(2)}) async-start(bf16[16,16,1152]{2,1,0:T(8,128)(2,1)} %get-tuple-element.100), calls=%async_computation.15 | async-start | bytes 1179648 | tf_op jit(solution)/shard_map/all_to_all | solution.py:597
  382.6 0.8 copy-start.3
  385.4 12.6 %all-to-all-start.15 = ((bf16[16,16,512]{2,1,0:T(8,128)(2,1)}), bf16[16,16,512]{2,1,0:T(8,128)(2,1)S(1)}, u32[]{:S(2)}, u32[]{:S(2)}) async-start(bf16[16,16,512]{2,1,0:T(8,128)(2,1)} %get-tuple-element.102), calls=%async_computation.16 | async-start | bytes 524288 | tf_op jit(solution)/shard_map/all_to_all | solution.py:597
  398.0 20.9 %all-to-all-start.16 = ((bf16[8,144,512]{2,1,0:T(8,128)(2,1)}), bf16[8,144,512]{2,1,0:T(8,128)(2,1)S(1)}, u32[]{:S(2)}, u32[]{:S(2)}) async-start(bf16[8,144,512]{2,1,0:T(8,128)(2,1)} %broadcast_dynamic-update-slice_fusion), calls=%async_computation.17 | async-start | bytes 2359296 | tf_op jit(solution)/shard_map/all_to_all | solution.py:786
  401.6 4.5 %collective-permute-start.14 = (bf16[64,512]{1,0:T(8,128)(2,1)S(1)}, bf16[64,512]{1,0:T(8,128)(2,1)S(1)}, u32[]{:S(2)}, u32[]{:S(2)}) collective-permute-start(bf16[64,512]{1,0:T(8,128)(2,1)S(1)} %fusion.2), channel_id=1, source_target_pairs={{0,8},{8,0},{1,9},{9,1},{2,10},{10,2},{3,11},{11,3},{4,12},{12,4},... | collective-permute-start | bytes 196616 | tf_op jit(solution)/shard_map/ppermute | solution.py:40
  421.2 6.5 %collective-permute-start.12 = (bf16[2,64,512]{2,1,0:T(8,128)(2,1)S(1)}, bf16[2,64,512]{2,1,0:T(8,128)(2,1)S(1)}, u32[]{:S(2)}, u32[]{:S(2)}) collective-permute-start(bf16[2,64,512]{2,1,0:T(8,128)(2,1)S(1)} %get-tuple-element.117), channel_id=1, source_target_pairs={{0,8},{8,0},{1,9},{9,1},{2,10},{10,2},{3,11},{11,3},{4,12},{12,4},... | collective-permute-start | bytes 393224 | tf_op jit(solution)/shard_map/ppermute | solution.py:40
  421.9 10.1 %collective-permute-start.11 = (bf16[2,64,1024]{2,1,0:T(8,128)(2,1)S(1)}, bf16[2,64,1024]{2,1,0:T(8,128)(2,1)S(1)}, u32[]{:S(2)}, u32[]{:S(2)}) collective-permute-start(bf16[2,64,1024]{2,1,0:T(8,128)(2,1)S(1)} %get-tuple-element.121), channel_id=1, source_target_pairs={{0,8},{8,0},{1,9},{9,1},{2,10},{10,2},{3,11},{11,3},{4,12},{12,4},... | collective-permute-start | bytes 786440 | tf_op jit(solution)/shard_map/ppermute | solution.py:40
  433.1 4.3 collective-permute-start.13
Sparse Core Ops, SparseCore 0:
  84.0 25.8 all-gather.2
  111.6 27.7 all-gather.4
  242.7 39.0 reduce-scatter.3
  284.0 31.9 reduce-scatter.7
  326.0 38.8 reduce-scatter.5
